TPU v7x, 32 devices: a whole 2x2x4 slice. The times are simulated.
32 devices in a mesh: blk: 8 (over z, x), head: 4 (over y, core).
Axes of the slice: x: 2, y: 2, z: 4, core: 2. Of those that a mesh axis runs over, the one named last changes fastest.
Arguments:
- queries: bfloat16 [4096, 1024], P(('blk', 'head')), may hold values from -6 to 6
- key_vectors: bfloat16 [4096, 1024], P(('blk', 'head')), may hold values from -6 to 6
- value_vectors: bfloat16 [4096, 1024], P(('blk', 'head')), may hold values from -6 to 6
- grad_output: bfloat16 [4096, 1024], P(('blk', 'head')), may hold values from -6 to 6
- lengths: int32 [4], replicated, may hold values from 1 to 2048, 4096 in all
Outputs:
- grad_queries: bfloat16 [4096, 1024], P(('blk', 'head'))
- grad_keys: bfloat16 [4096, 1024], P(('blk', 'head'))
- grad_values: bfloat16 [4096, 1024], P(('blk', 'head'))
Inputs may be any that keep to these rules, and one draw needn't show every extreme that they name: 4 positive lengths that sum to 4096; the longest is exactly 2048.
All inputs are finite; a program needn't handle non-finite values.
Results may differ from a plain program's by a relative error of at most 0.0086.
Values may be sent and summed in bfloat16 or wider, within the bound.
No kernel may reach another device: no remote copies, remote signals or barrier semaphores. Data moves between devices by JAX's collectives and lax.ppermute only.
A program may use at most 64 MiB of HBM per device.

v0:
```python
import jax
import jax.numpy as jnp
from jax import lax
from jax.sharding import PartitionSpec as P

DH = 64
WIN = 64


def with_halo(block, sides, width):
    for axis, dim in sides:
        count = lax.axis_size(axis)
        forward = [(i, i + 1) for i in range(count - 1)]
        backward = [(target, source) for source, target in forward]
        low = lax.ppermute(
            lax.slice_in_dim(block, block.shape[dim] - width, None, axis=dim), axis, forward
        )
        high = lax.ppermute(lax.slice_in_dim(block, 0, width, axis=dim), axis, backward)
        block = jnp.concatenate([low, block, high], axis=dim)
    return block


def shifted(block, axis, distance):
    devices = range(lax.axis_size(axis))
    route = [(i - distance, i) for i in devices if i - distance in devices]
    return lax.ppermute(block, axis, route)


def recording_of(positions, rec_ends):
    return jnp.sum((rec_ends[None, :] <= positions[:, None]).astype(jnp.int32), axis=1)


def band_grads(query_rows, grad_rows, key_value, query_first, key_first, rec_ends, frames):
    row_count = query_rows.shape[0]
    columns = query_rows.shape[1]
    head_count = columns // DH
    step_rows = min(512, 2 * WIN)
    key_span = step_rows + 2 * WIN
    score_scale = DH ** (-0.5)
    pair_grad = jnp.zeros((key_value.shape[0], 2 * columns), jnp.float32)
    query_parts = []
    for first_row in range(0, row_count, step_rows):
        query_block = query_rows[first_row : first_row + step_rows].reshape(
            step_rows, head_count, DH
        )
        grad_block = grad_rows[first_row : first_row + step_rows].reshape(step_rows, head_count, DH)
        pair_block = key_value[first_row : first_row + key_span]
        key_block = pair_block[:, :columns].reshape(key_span, head_count, DH)
        value_block = pair_block[:, columns:].reshape(key_span, head_count, DH)
        query_pos = query_first + first_row + jnp.arange(step_rows, dtype=jnp.int32)
        key_pos = key_first + first_row + jnp.arange(key_span, dtype=jnp.int32)
        inside = (key_pos >= 0) & (key_pos < frames)
        visible = jnp.abs(query_pos[:, None] - key_pos[None, :]) <= WIN
        visible = visible & (
            recording_of(query_pos, rec_ends)[:, None] == recording_of(key_pos, rec_ends)[None, :]
        )
        visible = visible & (inside[None, :] | (query_pos[:, None] == key_pos[None, :]))
        scores = (
            jnp.einsum("qhd,khd->hqk", query_block, key_block, preferred_element_type=jnp.float32)
            * score_scale
        )
        scores = jnp.where(visible[None], scores, -1e30)
        row_max = jnp.max(scores, axis=-1, keepdims=True)
        weights = jnp.where(visible[None], jnp.exp(scores - row_max), 0.0)
        probs = weights / jnp.sum(weights, axis=-1, keepdims=True)
        probs_low = probs.astype(jnp.bfloat16)
        value_part = jnp.einsum(
            "hqk,qhd->khd", probs_low, grad_block, preferred_element_type=jnp.float32
        )
        prob_grad = jnp.einsum(
            "qhd,khd->hqk", grad_block, value_block, preferred_element_type=jnp.float32
        )
        row_delta = jnp.sum(probs * prob_grad, axis=-1, keepdims=True)
        score_grad = (probs * (prob_grad - row_delta) * score_scale).astype(jnp.bfloat16)
        query_grad = jnp.einsum(
            "hqk,khd->qhd", score_grad, key_block, preferred_element_type=jnp.float32
        )
        key_part = jnp.einsum(
            "hqk,qhd->khd", score_grad, query_block, preferred_element_type=jnp.float32
        )
        both_parts = jnp.concatenate(
            [key_part.reshape(key_span, columns), value_part.reshape(key_span, columns)], axis=1
        )
        pair_grad = pair_grad.at[first_row : first_row + key_span].add(both_parts)
        query_parts.append(query_grad.reshape(step_rows, columns))
    return (jnp.concatenate(query_parts, axis=0), pair_grad)


def body(queries, key_vectors, value_vectors, grad_output, lengths):
    group_size = lax.axis_size("head")
    block_rows = queries.shape[0] * group_size
    columns = queries.shape[1] // group_size
    frames = block_rows * lax.axis_size("blk")
    head_queries, head_keys, head_values, head_grads = (
        lax.all_to_all(queries, "head", split_axis=1, concat_axis=0, tiled=True),
        lax.all_to_all(key_vectors, "head", split_axis=1, concat_axis=0, tiled=True),
        lax.all_to_all(value_vectors, "head", split_axis=1, concat_axis=0, tiled=True),
        lax.all_to_all(grad_output, "head", split_axis=1, concat_axis=0, tiled=True),
    )
    key_value = jnp.concatenate([head_keys, head_values], axis=1)
    rec_ends = jnp.cumsum(lengths)
    base_pos = lax.axis_index("blk") * block_rows
    extended = with_halo(key_value, (("blk", 0),), WIN)
    query_grad, pair_grad = band_grads(
        head_queries, head_grads, extended, base_pos, base_pos - WIN, rec_ends, frames
    )
    own_rows = pair_grad[WIN : WIN + block_rows]
    arrived = []
    for step_by, rim_rows in ((1, pair_grad[WIN + block_rows :]), (-1, pair_grad[:WIN])):
        arrived.append(shifted(rim_rows, "blk", step_by))
    own_rows = own_rows.at[:WIN].add(arrived[0]).at[block_rows - WIN :].add(arrived[1])
    outputs = (
        lax.all_to_all(
            query_grad.astype(jnp.bfloat16), "head", split_axis=0, concat_axis=1, tiled=True
        ),
        lax.all_to_all(
            own_rows[:, :columns].astype(jnp.bfloat16),
            "head",
            split_axis=0,
            concat_axis=1,
            tiled=True,
        ),
        lax.all_to_all(
            own_rows[:, columns:].astype(jnp.bfloat16),
            "head",
            split_axis=0,
            concat_axis=1,
            tiled=True,
        ),
    )
    return (outputs[0], outputs[1], outputs[2])


def solution(mesh):
    return jax.shard_map(
        body,
        mesh=mesh,
        in_specs=(
            P(("blk", "head"), None),
            P(("blk", "head"), None),
            P(("blk", "head"), None),
            P(("blk", "head"), None),
            P(),
        ),
        out_specs=(P(("blk", "head"), None), P(("blk", "head"), None), P(("blk", "head"), None)),
        check_vma=False,
    )
```

profile of v0, /device:TPU:25, one launch (start us, length us, event | category | flops | bytes accessed | tf_op | source)
XLA Modules:
  0.0 103.6 jit_solution(3987964290970095193)
XLA Ops:
  0.7 1.2 %copy.101 = bf16[128,1024]{0,1:T(8,128)(2,1)S(1)} copy(bf16[128,1024]{1,0:T(8,128)(2,1)} %param.18) | data formatting | bytes 524288 | tf_op args[1]
  1.8 0.9 copy.102
  2.7 4.0 %all-to-all-start = ((bf16[128,4,256]{2,0,1:T(8,128)(2,1)}), bf16[128,4,256]{2,0,1:T(8,128)(2,1)S(1)}, u32[]{:S(2)}, u32[]{:S(2)}) async-start(bf16[128,4,256]{2,0,1:T(8,128)(2,1)} %copy.102), calls=%async_computation | async-start | bytes 524288 | tf_op jit(solution)/shard_map/all_to_all | solution.py:96
  6.8 0.8 copy.156
  7.8 0.9 copy.104
  8.7 0.2 reduce-window.8
  9.1 0.2 fusion.87
  9.2 0.8 fusion.86
  10.0 1.9 %all-to-all-done = bf16[128,4,256]{2,0,1:T(8,128)(2,1)S(1)} async-done(((bf16[128,4,256]{2,0,1:T(8,128)(2,1)}), bf16[128,4,256]{2,0,1:T(8,128)(2,1)S(1)}, u32[]{:S(2)}, u32[]{:S(2)}) %all-to-all-start) | async-done | bytes 262176 | tf_op jit(solution)/shard_map/all_to_all | solution.py:96
  11.9 4.2 %all-to-all-start.1 = ((bf16[128,4,256]{2,0,1:T(8,128)(2,1)}), bf16[128,4,256]{2,0,1:T(8,128)(2,1)S(1)}, u32[]{:S(2)}, u32[]{:S(2)}) async-start(bf16[128,4,256]{2,0,1:T(8,128)(2,1)} %copy.104), calls=%async_computation.1 | async-start | bytes 524288 | tf_op jit(solution)/shard_map/all_to_all | solution.py:97
  16.2 0.8 fusion.85
  16.9 4.4 %all-to-all-done.1 = bf16[128,4,256]{2,0,1:T(8,128)(2,1)S(1)} async-done(((bf16[128,4,256]{2,0,1:T(8,128)(2,1)}), bf16[128,4,256]{2,0,1:T(8,128)(2,1)S(1)}, u32[]{:S(2)}, u32[]{:S(2)}) %all-to-all-start.1) | async-done | bytes 262176 | tf_op jit(solution)/shard_map/all_to_all | solution.py:97
  21.3 4.2 %all-to-all-start.2 = ((bf16[128,4,256]{0,2,1:T(8,128)(2,1)}), bf16[128,4,256]{0,2,1:T(8,128)(2,1)S(1)}, u32[]{:S(2)}, u32[]{:S(2)}) async-start(bf16[128,4,256]{0,2,1:T(8,128)(2,1)} %bitcast.9), calls=%async_computation.2 | async-start | bytes 524288 | tf_op jit(solution)/shard_map/all_to_all | solution.py:95
  25.6 0.2 fusion.84
  25.8 0.8 copy.157
  27.0 3.1 %collective-permute-start = (bf16[64,512]{0,1:T(8,128)(2,1)S(1)}, bf16[64,512]{0,1:T(8,128)(2,1)S(1)}, u32[]{:S(2)}, u32[]{:S(2)}) collective-permute-start(bf16[64,512]{0,1:T(8,128)(2,1)S(1)} %get-tuple-element.101), channel_id=1, source_target_pairs={{0,4},{4,8},{8,12},{12,16},{16,20},{20,24},{24,28},{1,5},{5,9},{9,... | collective-permute-start | bytes 196616 | tf_op jit(solution)/shard_map/ppermute | solution.py:15
  30.1 3.1 %collective-permute-start.1 = (bf16[64,512]{0,1:T(8,128)(2,1)S(1)}, bf16[64,512]{0,1:T(8,128)(2,1)S(1)}, u32[]{:S(2)}, u32[]{:S(2)}) collective-permute-start(bf16[64,512]{0,1:T(8,128)(2,1)S(1)} %get-tuple-element.102), channel_id=1, source_target_pairs={{4,0},{8,4},{12,8},{16,12},{20,16},{24,20},{28,24},{5,1},{9,5},{13... | collective-permute-start | bytes 196616 | tf_op jit(solution)/shard_map/ppermute | solution.py:18
  33.2 4.0 %all-to-all-start.3 = ((bf16[128,4,256]{0,2,1:T(8,128)(2,1)}), bf16[128,4,256]{0,2,1:T(8,128)(2,1)S(1)}, u32[]{:S(2)}, u32[]{:S(2)}) async-start(bf16[128,4,256]{0,2,1:T(8,128)(2,1)} %bitcast.14), calls=%async_computation.3 | async-start | bytes 524288 | tf_op jit(solution)/shard_map/all_to_all | solution.py:98
  37.2 5.1 %all-to-all-done.3 = bf16[128,4,256]{0,2,1:T(8,128)(2,1)S(1)} async-done(((bf16[128,4,256]{0,2,1:T(8,128)(2,1)}), bf16[128,4,256]{0,2,1:T(8,128)(2,1)S(1)}, u32[]{:S(2)}, u32[]{:S(2)}) %all-to-all-start.3) | async-done | bytes 262176 | tf_op jit(solution)/shard_map/all_to_all | solution.py:98
  42.4 0.5 pad_maximum_fusion.5
  43.0 0.3 convolution_bitcast_fusion.1
  43.2 0.4 fusion.123
  43.7 0.9 convolution_convert_fusion.3
  44.6 0.3 fusion.42
  44.9 0.6 fusion.70
  45.4 0.3 convolution_bitcast_fusion
  45.7 0.4 fusion.120
  46.1 0.9 convolution_convert_fusion.2
  47.1 1.0 fusion.45
  48.1 1.3 %fusion.64 = f32[4,256,64]{1,2,0:T(8,128)} fusion(bf16[128,4,64]{0,2,1:T(8,128)(2,1)S(1)} %bitcast.172, f32[4,128]{1,0:T(4,128)S(1)} %get-tuple-element.115, pred[128,256]{0,1:T(8,128)(4,1)S(1)} %fusion.84, bf16[256,4,64]{0,2,1:T(8,128)(2,1)S(1)} %bitcast.183, bf16[128,4,64]{0,2,1:T(8,128)(2,1)S(1)} %bitcast.197), kind=kOutput, calls=%fused_computation.78 | convolution fusion | flops 34341632 | bytes 559104 | tf_op jit(solution)/shard_map/hqk,qhd->khd/dot_general | solution.py:67
  49.4 0.3 fusion.125
  49.6 1.2 %fusion.121 = (f32[4,128]{1,0:T(4,128)S(1)}, f32[4,128,256]{1,2,0:T(8,128)}) fusion(bf16[128,4,64]{0,2,1:T(8,128)(2,1)S(1)} %bitcast.191, bf16[256,4,64]{0,2,1:T(8,128)(2,1)S(1)} %bitcast.178, pred[128,256]{0,1:T(8,128)(4,1)S(1)} %copy-done.16), kind=kOutput, calls=%fused_computation.172 | convolution fusion | flops 17432832 | bytes 755712 | tf_op jit(solution)/shard_map/sub | solution.py:64
  50.8 0.6 fusion.66
  51.4 0.3 fusion.124
  51.7 0.4 fusion.122
  52.1 1.3 %fusion.68 = f32[4,256,64]{1,2,0:T(8,128)} fusion(bf16[128,4,64]{0,2,1:T(8,128)(2,1)S(1)} %bitcast.168, f32[4,128]{1,0:T(4,128)S(1)} %get-tuple-element.119, pred[128,256]{0,1:T(8,128)(4,1)S(1)} %copy-done.15, bf16[128,4,64]{0,2,1:T(8,128)(2,1)S(1)} %bitcast.189, bf16[256,4,64]{0,2,1:T(8,128)(2,1)S(1)} %bitcast.176), kind=kOutput, calls=%fused_computation.82 | convolution fusion | flops 34341632 | bytes 559104 | tf_op jit(solution)/shard_map/hqk,qhd->khd/dot_general | solution.py:67
  53.4 1.5 %fusion.44 = f32[4,256,64]{1,2,0:T(8,128)S(1)} fusion(bf16[128,4,64]{0,2,1:T(8,128)(2,1)S(1)} %bitcast.193, f32[4,128,256]{1,2,0:T(8,128)S(1)} %fusion.125, f32[4,128,256]{1,2,0:T(8,128)} %get-tuple-element.118, f32[4,128]{1,0:T(4,128)S(1)} %get-tuple-element.117), kind=kOutput, calls=%fused_computation.56 | convolution fusion | flops 17695488 | bytes 1378304 | tf_op jit(solution)/shard_map/hqk,qhd->khd/dot_general | solution.py:78
  55.0 1.0 fusion.43
  56.1 0.9 copy-done.3
  57.2 0.7 copy-done.5
  58.0 0.2 constant_dynamic-update-slice_fusion
  58.3 2.2 %collective-permute-start.2 = (f32[64,512]{0,1:T(8,128)S(1)}, f32[64,512]{0,1:T(8,128)S(1)}, u32[]{:S(2)}, u32[]{:S(2)}) collective-permute-start(f32[64,512]{0,1:T(8,128)S(1)} %slice.255), channel_id=1, source_target_pairs={{0,4},{4,8},{8,12},{12,16},{16,20},{20,24},{24,28},{1,5},{5,9},{9,... | collective-permute-start | bytes 393224 | tf_op jit(solution)/shard_map/ppermute | solution.py:26
  60.6 1.5 %convolution_convert_fusion = bf16[4,128,64]{1,2,0:T(8,128)(2,1)S(1)} fusion(bf16[256,4,64]{0,2,1:T(8,128)(2,1)S(1)} %bitcast.180, f32[4,128,256]{1,2,0:T(8,128)S(1)} %fusion.125, f32[4,128,256]{1,2,0:T(8,128)} %get-tuple-element.118, f32[4,128]{1,0:T(4,128)S(1)} %get-tuple-element.117), kind=kOutput, calls=%fused_computation.50 | convolution fusion | flops 17728256 | bytes 1247232 | tf_op jit(solution)/shard_map/hqk,khd->qhd/dot_general | solution.py:75
  62.1 6.0 %collective-permute-done.2 = f32[64,512]{0,1:T(8,128)S(1)} collective-permute-done((f32[64,512]{0,1:T(8,128)S(1)}, f32[64,512]{0,1:T(8,128)S(1)}, u32[]{:S(2)}, u32[]{:S(2)}) %collective-permute-start.2) | collective-permute-done | bytes 131104 | tf_op jit(solution)/shard_map/ppermute | solution.py:26
  68.2 1.9 %collective-permute-start.3 = (f32[64,512]{0,1:T(8,128)S(1)}, f32[64,512]{0,1:T(8,128)S(1)}, u32[]{:S(2)}, u32[]{:S(2)}) collective-permute-start(f32[64,512]{0,1:T(8,128)S(1)} %get-tuple-element.91), channel_id=1, source_target_pairs={{4,0},{8,4},{12,8},{16,12},{20,16},{24,20},{28,24},{5,1},{9,5},{13... | collective-permute-start | bytes 393224 | tf_op jit(solution)/shard_map/ppermute | solution.py:26
  70.2 1.5 %convolution_convert_fusion.1 = bf16[4,128,64]{1,2,0:T(8,128)(2,1)S(1)} fusion(bf16[256,4,64]{0,2,1:T(8,128)(2,1)S(1)} %bitcast.177, f32[4,128,256]{1,2,0:T(8,128)S(1)} %fusion.124, f32[4,128,256]{1,2,0:T(8,128)} %copy-done.18, f32[4,128]{1,0:T(4,128)S(1)} %get-tuple-element.119), kind=kOutput, calls=%fused_computation.51 | convolution fusion | flops 17728256 | bytes 1247232 | tf_op jit(solution)/shard_map/hqk,khd->qhd/dot_general | solution.py:75
  71.7 0.3 slice.253
  72.0 0.5 copy-done.9
  72.6 0.8 copy.123
  73.4 5.1 %all-to-all-start.4 = ((bf16[4,128,256]{2,1,0:T(8,128)(2,1)}), bf16[4,128,256]{2,1,0:T(8,128)(2,1)S(1)}, u32[]{:S(2)}, u32[]{:S(2)}) async-start(bf16[4,128,256]{2,1,0:T(8,128)(2,1)} %bitcast.42), calls=%async_computation.4 | async-start | bytes 524288 | tf_op jit(solution)/shard_map/all_to_all | solution.py:113
  78.6 1.9 %scatter-add.26 = f32[512,512]{0,1:T(8,128)S(1)} dynamic-update-slice(f32[512,512]{0,1:T(8,128)S(1)} %slice.253, f32[64,512]{0,1:T(8,128)S(1)} %get-tuple-element.92, s32[]{:T(128)} %constant.187.clone.1, s32[]{:T(128)} %constant.187.clone.1) | dynamic-update-slice | bytes 262148 | tf_op jit(solution)/shard_map/scatter-add | solution.py:111
  80.6 1.5 %scatter-add.29 = f32[512,512]{0,1:T(8,128)S(1)} dynamic-update-slice(f32[512,512]{0,1:T(8,128)S(1)} %scatter-add.26, f32[64,512]{0,1:T(8,128)S(1)} %slice_add_fusion.3, s32[]{:T(128)} %constant.198.clone.1, s32[]{:T(128)} %constant.187.clone.1) | dynamic-update-slice | bytes 262148 | tf_op jit(solution)/shard_map/scatter-add | solution.py:111
  82.2 0.8 copy.135
  83.0 0.7 all-to-all-done.4
  83.7 4.2 %all-to-all-start.6 = ((bf16[4,128,256]{2,1,0:T(8,128)(2,1)}), bf16[4,128,256]{2,1,0:T(8,128)(2,1)S(1)}, u32[]{:S(2)}, u32[]{:S(2)}) async-start(bf16[4,128,256]{2,1,0:T(8,128)(2,1)} %bitcast.64), calls=%async_computation.6 | async-start | bytes 524288 | tf_op jit(solution)/shard_map/all_to_all | solution.py:123
  88.0 0.8 copy.133
  88.8 4.3 %all-to-all-done.6 = bf16[4,128,256]{2,1,0:T(8,128)(2,1)S(1)} async-done(((bf16[4,128,256]{2,1,0:T(8,128)(2,1)}), bf16[4,128,256]{2,1,0:T(8,128)(2,1)S(1)}, u32[]{:S(2)}, u32[]{:S(2)}) %all-to-all-start.6) | async-done | bytes 262176 | tf_op jit(solution)/shard_map/all_to_all | solution.py:123
  93.2 4.2 %all-to-all-start.5 = ((bf16[4,128,256]{2,1,0:T(8,128)(2,1)}), bf16[4,128,256]{2,1,0:T(8,128)(2,1)S(1)}, u32[]{:S(2)}, u32[]{:S(2)}) async-start(bf16[4,128,256]{2,1,0:T(8,128)(2,1)} %bitcast.61), calls=%async_computation.5 | async-start | bytes 524288 | tf_op jit(solution)/shard_map/all_to_all | solution.py:116
  97.6 0.9 copy.137
  98.4 0.2 copy.136
  98.6 0.9 copy.139
  99.5 3.1 %all-to-all-done.5 = bf16[4,128,256]{2,1,0:T(8,128)(2,1)S(1)} async-done(((bf16[4,128,256]{2,1,0:T(8,128)(2,1)}), bf16[4,128,256]{2,1,0:T(8,128)(2,1)S(1)}, u32[]{:S(2)}, u32[]{:S(2)}) %all-to-all-start.5) | async-done | bytes 262176 | tf_op jit(solution)/shard_map/all_to_all | solution.py:116
  102.6 0.2 copy.134
  102.7 0.9 copy.138
  (63 shorter events, 2.1 us)
Async XLA Ops:
  0.6 6.2 %copy-start = (bf16[128,1024]{1,0:T(8,128)(2,1)S(1)}, bf16[128,1024]{1,0:T(8,128)(2,1)}, u32[]{:S(2)}) copy-start(bf16[128,1024]{1,0:T(8,128)(2,1)} %param.17) | copy-start | bytes 786436
  0.6 7.0 %copy-start.1 = (bf16[128,1024]{1,0:T(8,128)(2,1)S(1)}, bf16[128,1024]{1,0:T(8,128)(2,1)}, u32[]{:S(2)}) copy-start(bf16[128,1024]{1,0:T(8,128)(2,1)} %param.19) | copy-start | bytes 786436
  1.8 6.9 %copy-start.17 = (s32[4]{0:T(128)S(1)}, s32[4]{0:T(128)}, u32[]{:S(2)}) copy-start(s32[4]{0:T(128)} %param.21) | copy-start | bytes 52
  2.7 9.2 %all-to-all-start = ((bf16[128,4,256]{2,0,1:T(8,128)(2,1)}), bf16[128,4,256]{2,0,1:T(8,128)(2,1)S(1)}, u32[]{:S(2)}, u32[]{:S(2)}) async-start(bf16[128,4,256]{2,0,1:T(8,128)(2,1)} %copy.102), calls=%async_computation | async-start | bytes 524288 | tf_op jit(solution)/shard_map/all_to_all | solution.py:96
  6.8 18.9 %copy-start.2 = (bf16[128,1024]{1,0:T(8,128)(2,1)S(1)}, bf16[128,1024]{1,0:T(8,128)(2,1)}, u32[]{:S(2)}) copy-start(bf16[128,1024]{1,0:T(8,128)(2,1)} %param.20) | copy-start | bytes 786436
  11.9 9.4 %all-to-all-start.1 = ((bf16[128,4,256]{2,0,1:T(8,128)(2,1)}), bf16[128,4,256]{2,0,1:T(8,128)(2,1)S(1)}, u32[]{:S(2)}, u32[]{:S(2)}) async-start(bf16[128,4,256]{2,0,1:T(8,128)(2,1)} %copy.104), calls=%async_computation.1 | async-start | bytes 524288 | tf_op jit(solution)/shard_map/all_to_all | solution.py:97
  21.3 11.9 %all-to-all-start.2 = ((bf16[128,4,256]{0,2,1:T(8,128)(2,1)}), bf16[128,4,256]{0,2,1:T(8,128)(2,1)S(1)}, u32[]{:S(2)}, u32[]{:S(2)}) async-start(bf16[128,4,256]{0,2,1:T(8,128)(2,1)} %bitcast.9), calls=%async_computation.2 | async-start | bytes 524288 | tf_op jit(solution)/shard_map/all_to_all | solution.py:95
  27.0 15.4 %collective-permute-start = (bf16[64,512]{0,1:T(8,128)(2,1)S(1)}, bf16[64,512]{0,1:T(8,128)(2,1)S(1)}, u32[]{:S(2)}, u32[]{:S(2)}) collective-permute-start(bf16[64,512]{0,1:T(8,128)(2,1)S(1)} %get-tuple-element.101), channel_id=1, source_target_pairs={{0,4},{4,8},{8,12},{12,16},{16,20},{20,24},{24,28},{1,5},{5,9},{9,... | collective-permute-start | bytes 196616 | tf_op jit(solution)/shard_map/ppermute | solution.py:15
  30.1 12.3 %collective-permute-start.1 = (bf16[64,512]{0,1:T(8,128)(2,1)S(1)}, bf16[64,512]{0,1:T(8,128)(2,1)S(1)}, u32[]{:S(2)}, u32[]{:S(2)}) collective-permute-start(bf16[64,512]{0,1:T(8,128)(2,1)S(1)} %get-tuple-element.102), channel_id=1, source_target_pairs={{4,0},{8,4},{12,8},{16,12},{20,16},{24,20},{28,24},{5,1},{9,5},{13... | collective-permute-start | bytes 196616 | tf_op jit(solution)/shard_map/ppermute | solution.py:18
  33.2 9.2 %all-to-all-start.3 = ((bf16[128,4,256]{0,2,1:T(8,128)(2,1)}), bf16[128,4,256]{0,2,1:T(8,128)(2,1)S(1)}, u32[]{:S(2)}, u32[]{:S(2)}) async-start(bf16[128,4,256]{0,2,1:T(8,128)(2,1)} %bitcast.14), calls=%async_computation.3 | async-start | bytes 524288 | tf_op jit(solution)/shard_map/all_to_all | solution.py:98
  37.2 13.6 %copy-start.12 = (bf16[1,128,256]{1,2,0:T(8,128)(2,1)}, bf16[1,128,256]{1,2,0:T(8,128)(2,1)S(1)}, u32[]{:S(2)}) copy-start(bf16[1,128,256]{1,2,0:T(8,128)(2,1)S(1)} %get-tuple-element.105) | copy-start | bytes 196612
  37.2 14.9 %copy-start.10 = (bf16[1,128,256]{1,2,0:T(8,128)(2,1)}, bf16[1,128,256]{1,2,0:T(8,128)(2,1)S(1)}, u32[]{:S(2)}) copy-start(bf16[1,128,256]{1,2,0:T(8,128)(2,1)S(1)} %get-tuple-element.106) | copy-start | bytes 196612
  42.9 7.9 %copy-start.7 = (bf16[256,256]{0,1:T(8,128)(2,1)}, bf16[256,256]{0,1:T(8,128)(2,1)S(1)}, u32[]{:S(2)}) copy-start(bf16[256,256]{0,1:T(8,128)(2,1)S(1)} %get-tuple-element.111) | copy-start | bytes 393220
  48.1 1.6 %copy-start.16 = (pred[128,256]{0,1:T(8,128)(4,1)S(1)}, pred[128,256]{0,1:T(8,128)(4,1)}, u32[]{:S(2)}) copy-start(pred[128,256]{0,1:T(8,128)(4,1)} %fusion.85) | copy-start | bytes 98308
  50.8 0.9 copy-start.15
  52.1 2.8 %copy-start.18 = (f32[4,128,256]{1,2,0:T(8,128)}, f32[4,128,256]{1,2,0:T(8,128)S(1)}, u32[]{:S(2)}) copy-start(f32[4,128,256]{1,2,0:T(8,128)S(1)} %get-tuple-element.120) | copy-start | bytes 1572868
  52.1 1.3 %copy-start.13 = (bf16[1,128,256]{1,2,0:T(8,128)(2,1)S(1)}, bf16[1,128,256]{1,2,0:T(8,128)(2,1)}, u32[]{:S(2)}) copy-start(bf16[1,128,256]{1,2,0:T(8,128)(2,1)} %copy-done.12) | copy-start | bytes 196612
  53.4 1.6 %copy-start.11 = (bf16[1,128,256]{1,2,0:T(8,128)(2,1)S(1)}, bf16[1,128,256]{1,2,0:T(8,128)(2,1)}, u32[]{:S(2)}) copy-start(bf16[1,128,256]{1,2,0:T(8,128)(2,1)} %copy-done.10) | copy-start | bytes 196612
  56.0 0.9 copy-start.3
  56.0 1.0 copy-start.4
  57.0 0.9 copy-start.5
  57.0 1.0 copy-start.6
  58.0 2.5 %copy-start.8 = (bf16[256,256]{0,1:T(8,128)(2,1)S(1)}, bf16[256,256]{0,1:T(8,128)(2,1)}, u32[]{:S(2)}) copy-start(bf16[256,256]{0,1:T(8,128)(2,1)} %copy-done.7) | copy-start | bytes 393220
  58.3 9.7 %collective-permute-start.2 = (f32[64,512]{0,1:T(8,128)S(1)}, f32[64,512]{0,1:T(8,128)S(1)}, u32[]{:S(2)}, u32[]{:S(2)}) collective-permute-start(f32[64,512]{0,1:T(8,128)S(1)} %slice.255), channel_id=1, source_target_pairs={{0,4},{4,8},{8,12},{12,16},{16,20},{20,24},{24,28},{1,5},{5,9},{9,... | collective-permute-start | bytes 393224 | tf_op jit(solution)/shard_map/ppermute | solution.py:26
  68.2 12.2 %collective-permute-start.3 = (f32[64,512]{0,1:T(8,128)S(1)}, f32[64,512]{0,1:T(8,128)S(1)}, u32[]{:S(2)}, u32[]{:S(2)}) collective-permute-start(f32[64,512]{0,1:T(8,128)S(1)} %get-tuple-element.91), channel_id=1, source_target_pairs={{4,0},{8,4},{12,8},{16,12},{20,16},{24,20},{28,24},{5,1},{9,5},{13... | collective-permute-start | bytes 393224 | tf_op jit(solution)/shard_map/ppermute | solution.py:26
  71.7 0.8 copy-start.9
  71.7 0.9 copy-start.14
  73.4 10.3 %all-to-all-start.4 = ((bf16[4,128,256]{2,1,0:T(8,128)(2,1)}), bf16[4,128,256]{2,1,0:T(8,128)(2,1)S(1)}, u32[]{:S(2)}, u32[]{:S(2)}) async-start(bf16[4,128,256]{2,1,0:T(8,128)(2,1)} %bitcast.42), calls=%async_computation.4 | async-start | bytes 524288 | tf_op jit(solution)/shard_map/all_to_all | solution.py:113
  83.7 9.4 %all-to-all-start.6 = ((bf16[4,128,256]{2,1,0:T(8,128)(2,1)}), bf16[4,128,256]{2,1,0:T(8,128)(2,1)S(1)}, u32[]{:S(2)}, u32[]{:S(2)}) async-start(bf16[4,128,256]{2,1,0:T(8,128)(2,1)} %bitcast.64), calls=%async_computation.6 | async-start | bytes 524288 | tf_op jit(solution)/shard_map/all_to_all | solution.py:123
  93.2 9.4 %all-to-all-start.5 = ((bf16[4,128,256]{2,1,0:T(8,128)(2,1)}), bf16[4,128,256]{2,1,0:T(8,128)(2,1)S(1)}, u32[]{:S(2)}, u32[]{:S(2)}) async-start(bf16[4,128,256]{2,1,0:T(8,128)(2,1)} %bitcast.61), calls=%async_computation.5 | async-start | bytes 524288 | tf_op jit(solution)/shard_map/all_to_all | solution.py:116
where the time goes:
time: 105 us; the launch traced here: 104 us
  starting transfers between devices  40.5 us (39%)
  waiting for transfers between devices  25.6 us (24%)
  local copies, waits for them, and re-layouts  16.8 us (16%)
  matrix products  15.9 us (15%)
  other arithmetic  3.78 us (4%)
  between operations  1.09 us (1%)
    unnamed x43, local copies, waits for them, and re-layouts  6.22 us
    ppermute x2, waiting for transfers between devices, shifted(): return lax.ppermute(block, axis, route)  6.01 us
    all_to_all x1, starting transfers between devices, body(): lax.all_to_all(query_grad.astype(jnp.bfloat16), 'head', split_axis=0, con...  5.14 us
    all_to_all x1, waiting for transfers between devices, body(): lax.all_to_all(grad_output, 'head', split_axis=1, concat_axis=0, tiled=True)  5.13 us
    dot_general x4, matrix products, band_grads(): jnp.einsum('hqk,khd->qhd', score_grad, key_block, preferred_element_type=...  4.84 us
    all_to_all x1, waiting for transfers between devices, body(): lax.all_to_all(value_vectors, 'head', split_axis=1, concat_axis=0, tiled=...  4.39 us
    all_to_all x1, waiting for transfers between devices, body(): lax.all_to_all(own_rows[:, columns:].astype(jnp.bfloat16), 'head', split_...  4.33 us
    all_to_all x1, starting transfers between devices, body(): lax.all_to_all(value_vectors, 'head', split_axis=1, concat_axis=0, tiled=...  4.25 us
  transfers between devices with their start and end apart: 11, of which 7 were waited for; matrix products, arithmetic and copies ran while one was open for 16% of the time, Pallas kernels for 0%

commit v1 on v0

v1 whole, which is shorter than its diff:
```python
import functools

import jax
import jax.numpy as jnp
from jax import lax
from jax.experimental import pallas as pl
from jax.experimental.pallas import tpu as pltpu
from jax.sharding import PartitionSpec as P

DH = 64
WIN = 64
PAIR = 2 * DH
SCALE = DH ** (-0.5)
NEG = -1e30
AXES = ("blk", "head")
F32 = jnp.float32
BF16 = jnp.bfloat16


def flat_index():
    return lax.axis_index("blk") * lax.axis_size("head") + lax.axis_index("head")


def recording_of(pos, len_ref):
    rec = jnp.where(pos < 0, -1, 0)
    end = jnp.int32(0)
    for r in range(len_ref.shape[0]):
        end = end + len_ref[r]
        rec = rec + jnp.where(pos >= end, 1, 0)
    return rec


def bias_of(key_first, query_first, keys, queries, lane_queries, len_ref):
    kpos = key_first + lax.broadcasted_iota(jnp.int32, (keys, queries), 0)
    qpos = query_first + lax.broadcasted_iota(jnp.int32, (keys, queries), 1) % lane_queries
    near = jnp.abs(kpos - qpos) <= WIN
    same = recording_of(kpos, len_ref) == recording_of(qpos, len_ref)
    return jnp.where(near & same, 0.0, NEG).astype(F32)


def split_heads(pair):
    lane = lax.broadcasted_iota(jnp.int32, pair.shape, 1)
    zero = jnp.zeros_like(pair)
    return jnp.concatenate([jnp.where(lane < DH, pair, zero), jnp.where(lane < DH, zero, pair)], axis=0)


def nt(a, b):
    return lax.dot_general(a, b, (((1,), (1,)), ((), ())), preferred_element_type=F32)


def nn(a, b):
    return lax.dot_general(a, b, (((1,), (0,)), ((), ())), preferred_element_type=F32)


def tn(a, b):
    return lax.dot_general(a, b, (((0,), (0,)), ((), ())), preferred_element_type=F32)


def local_kernel(len_ref, q_ref, k_ref, v_ref, g_ref, qg_o, st_o, qg_e, st_e):
    rows, cols = q_ref.shape
    me = flat_index()
    odd = lax.rem(me, 2)
    base = me * rows
    half = rows // 2
    for out, first in ((qg_o, odd * half), (qg_e, (1 - odd) * half)):
        first = pl.multiple_of(first, half)
        out[:half, :] = q_ref[pl.ds(first, half), :]
        out[half:, :] = g_ref[pl.ds(first, half), :]
    bias = bias_of(base, base, rows, rows, rows, len_ref)
    bias = jnp.concatenate([bias, bias], axis=1)
    lane = lax.broadcasted_iota(jnp.int32, (1, rows), 1)
    for p in range(cols // PAIR):
        cs = slice(p * PAIR, (p + 1) * PAIR)
        qq = split_heads(q_ref[:, cs]) * BF16(SCALE)
        gg = split_heads(g_ref[:, cs])
        s = nt(k_ref[:, cs], qq) + bias
        dp = nt(v_ref[:, cs], gg)
        m = jnp.max(s, axis=0, keepdims=True)
        e = jnp.exp(s - m)
        l = jnp.sum(e, axis=0, keepdims=True)
        d = jnp.sum(e * dp, axis=0, keepdims=True)
        for n, stat in enumerate((m, l, d)):
            a, b = stat[:, :rows], stat[:, rows:]
            lo = jnp.where(lane < half, a, pltpu.roll(b, half, 1))
            hi = jnp.where(lane < half, pltpu.roll(a, half, 1), b)
            r = 3 * p + n
            st_o[r : r + 1, :] = jnp.where(odd == 1, hi, lo)
            st_e[r : r + 1, :] = jnp.where(odd == 1, lo, hi)


def own_kernel(len_ref, q_ref, k_ref, v_ref, g_ref, kv_o, kv_e, dq_ref, dk_ref, dv_ref, kx, vx):
    rows, cols = q_ref.shape
    me = flat_index()
    odd = lax.rem(me, 2)
    base = me * rows
    half = rows // 2
    for dst, own, o in ((kx, k_ref, 0), (vx, v_ref, half)):
        dst[half : half + rows, :] = own[...]

        @pl.when(odd == 1)
        def _():
            dst[:half, :] = kv_e[o : o + half, :]
            dst[half + rows :, :] = kv_o[o : o + half, :]

        @pl.when(odd == 0)
        def _():
            dst[:half, :] = kv_o[o : o + half, :]
            dst[half + rows :, :] = kv_e[o : o + half, :]

    span = rows + 2 * half
    bias = bias_of(base - half, base, span, rows, rows, len_ref)
    bias = jnp.concatenate([bias, bias], axis=1)
    lane = lax.broadcasted_iota(jnp.int32, (rows, PAIR), 1)
    for p in range(cols // PAIR):
        cs = slice(p * PAIR, (p + 1) * PAIR)
        qq = split_heads(q_ref[:, cs]) * BF16(SCALE)
        gg = split_heads(g_ref[:, cs])
        kp = kx[:, cs]
        s = nt(kp, qq) + bias
        dp = nt(vx[:, cs], gg)
        m = jnp.max(s, axis=0, keepdims=True)
        e = jnp.exp(s - m)
        inv = 1.0 / jnp.sum(e, axis=0, keepdims=True)
        prob = e * inv
        delta = jnp.sum(prob * dp, axis=0, keepdims=True)
        ds = (prob * (dp - delta)).astype(BF16)
        dv_ref[:, cs] = nn(prob[half : half + rows].astype(BF16), gg)
        dk_ref[:, cs] = nn(ds[half : half + rows], qq)
        dq2 = tn(ds, kp)
        dq_ref[:, cs] = (jnp.where(lane < DH, dq2[:rows], dq2[rows:]) * SCALE).astype(BF16)


def edge_kernel(len_ref, k_ref, v_ref, qg_o, st_o, qg_e, st_e, dka_ref, dva_ref, dk_ref, dv_ref, qg, st):
    rows, cols = k_ref.shape
    me = flat_index()
    odd = lax.rem(me, 2)
    base = me * rows
    half = rows // 2

    @pl.when(odd == 1)
    def _():
        qg[0], qg[1] = qg_e[...], qg_o[...]
        st[0], st[1] = st_e[...], st_o[...]

    @pl.when(odd == 0)
    def _():
        qg[0], qg[1] = qg_o[...], qg_e[...]
        st[0], st[1] = st_o[...], st_e[...]

    biases = (
        bias_of(base, base - half, half, 2 * half, half, len_ref),
        bias_of(base + half, base + rows, half, 2 * half, half, len_ref),
    )
    for p in range(cols // PAIR):
        cs = slice(p * PAIR, (p + 1) * PAIR)
        for side in range(2):
            rs = slice(side * half, (side + 1) * half)
            qq = split_heads(qg[side, :half, cs]) * BF16(SCALE)
            gg = split_heads(qg[side, half:, cs])
            m0 = st[side, 3 * p : 3 * p + 1, :]
            l0 = st[side, 3 * p + 1 : 3 * p + 2, :]
            d0 = st[side, 3 * p + 2 : 3 * p + 3, :]
            s = nt(k_ref[rs, cs], qq) + biases[side]
            dp = nt(v_ref[rs, cs], gg)
            m = jnp.maximum(m0, jnp.max(s, axis=0, keepdims=True))
            e = jnp.exp(s - m)
            a = jnp.exp(m0 - m)
            l = a * l0 + jnp.sum(e, axis=0, keepdims=True)
            d = a * d0 + jnp.sum(e * dp, axis=0, keepdims=True)
            inv = 1.0 / jnp.maximum(l, 1.0)
            prob = e * inv
            ds = (prob * (dp - d * inv)).astype(BF16)
            dv_ref[rs, cs] = (dva_ref[rs, cs] + nn(prob.astype(BF16), gg)).astype(BF16)
            dk_ref[rs, cs] = (dka_ref[rs, cs] + nn(ds, qq)).astype(BF16)


VM = pl.BlockSpec(memory_space=pltpu.VMEM)
SM = pl.BlockSpec(memory_space=pltpu.SMEM)


def body(queries, key_vectors, value_vectors, grad_output, lengths):
    rows, cols = queries.shape
    half = rows // 2
    count = lax.axis_size("blk") * lax.axis_size("head")
    odd = lax.rem(flat_index(), 2)
    across = [(a, b) for i in range(1, count - 1, 2) for a, b in ((i, i + 1), (i + 1, i))]
    within = [(a, b) for i in range(0, count, 2) for a, b in ((i, i + 1), (i + 1, i))]

    def edges(arrays, side):
        return jnp.concatenate([lax.dynamic_slice_in_dim(x, side * half, half, 0) for x in arrays], axis=0)

    kv_o = lax.ppermute(edges((key_vectors, value_vectors), odd), AXES, across)
    kv_e = lax.ppermute(edges((key_vectors, value_vectors), 1 - odd), AXES, within)
    stats = 3 * (cols // PAIR)
    sds = jax.ShapeDtypeStruct
    params = pltpu.CompilerParams(vmem_limit_bytes=20 << 20)
    qg_o, st_o, qg_e, st_e = pl.pallas_call(
        local_kernel,
        out_shape=(sds((rows, cols), BF16), sds((stats, rows), F32)) * 2,
        in_specs=[SM] + [VM] * 4,
        out_specs=(VM,) * 4,
        compiler_params=params,
        cost_estimate=pl.CostEstimate(flops=1 << 28, bytes_accessed=2 << 20, transcendentals=1 << 18),
    )(lengths, queries, key_vectors, value_vectors, grad_output)
    qg_o, st_o = lax.ppermute(qg_o, AXES, across), lax.ppermute(st_o, AXES, across)
    qg_e, st_e = lax.ppermute(qg_e, AXES, within), lax.ppermute(st_e, AXES, within)
    dq, dk, dv = pl.pallas_call(
        own_kernel,
        out_shape=(sds((rows, cols), BF16), sds((rows, cols), F32), sds((rows, cols), F32)),
        in_specs=[SM] + [VM] * 6,
        out_specs=(VM,) * 3,
        scratch_shapes=[pltpu.VMEM((2 * rows, cols), BF16)] * 2,
        compiler_params=params,
        cost_estimate=pl.CostEstimate(flops=1 << 30, bytes_accessed=4 << 20, transcendentals=1 << 19),
    )(lengths, queries, key_vectors, value_vectors, grad_output, kv_o, kv_e)
    dk, dv = pl.pallas_call(
        edge_kernel,
        out_shape=(sds((rows, cols), BF16),) * 2,
        in_specs=[SM] + [VM] * 8,
        out_specs=(VM,) * 2,
        scratch_shapes=[pltpu.VMEM((2, rows, cols), BF16), pltpu.VMEM((2, stats, rows), F32)],
        compiler_params=params,
        cost_estimate=pl.CostEstimate(flops=1 << 27, bytes_accessed=2 << 20, transcendentals=1 << 17),
    )(lengths, key_vectors, value_vectors, qg_o, st_o, qg_e, st_e, dk, dv)
    return dq, dk, dv


def solution(mesh):
    return jax.shard_map(
        body,
        mesh=mesh,
        in_specs=(P(AXES, None),) * 4 + (P(),),
        out_specs=(P(AXES, None),) * 3,
        check_vma=False,
    )
```

time: 105 us -> 25.6 us (0.24); the launches traced: 104 us -> 25.4 us
  starting transfers between devices: 40.5 us -> 12.7 us
  waiting for transfers between devices: 25.6 us -> 0.02 us
  matrix products: 15.9 us -> 0 us
  local copies, waits for them, and re-layouts: 16.8 us -> 1.42 us
  Pallas kernels: 0 us -> 10.5 us
  other arithmetic: 3.78 us -> 0.04 us
    all_to_all x7 -> x0, starting transfers between devices: 30.2 us -> none  [the longest x1 5.14 us: body(): lax.all_to_all(query_grad.astype(jnp.bfloat16), 'head', split_axis=0, con...]
    all_to_all x7 -> x0, waiting for transfers between devices: 19.6 us -> none  [the longest x1 5.13 us: body(): lax.all_to_all(grad_output, 'head', split_axis=1, concat_axis=0, tiled=True)]
    dot_general x16 -> x0, matrix products: 13.5 us -> none  [the longest x4 4.84 us: band_grads(): jnp.einsum('hqk,khd->qhd', score_grad, key_block, preferred_element_type=...]
    pallas_call x0 -> x3, Pallas kernels: none -> 10.5 us  [the longest x1 4.86 us: body(): pl.pallas_call(edge_kernel, out_shape=(sds((rows, cols), BF16),) * 2, in_...]
    ppermute x4 -> x6, waiting for transfers between devices: 6.01 us -> 0.02 us  [the longest x1 0.01 us: body(): kv_o = lax.ppermute(edges((key_vectors, value_vectors), odd), AXES, across)]
    unnamed x43 -> x10, local copies, waits for them, and re-layouts: 6.22 us -> 0.29 us
    all_to_all x9 -> x0, local copies, waits for them, and re-layouts: 4.17 us -> none  [the longest x2 1 us: body(): lax.all_to_all(value_vectors, 'head', split_axis=1, concat_axis=0, tiled=...]
    scatter-add x2 -> x0, local copies, waits for them, and re-layouts: 3.31 us -> none  [body(): own_rows.at[:WIN].add(arrived[0]).at[block_rows - WIN:].add(arrived[1])]
  transfers between devices with their start and end apart: 11 -> 6, of which waited for: 7 -> 0; matrix products, arithmetic and copies ran while one was open for 16% -> 0% of each run, Pallas kernels for 0% -> 22%
where the time goes in v1:
time: 25.6 us; the launch traced here: 25.4 us
  starting transfers between devices  12.7 us (50%)
  Pallas kernels  10.5 us (41%)
  local copies, waits for them, and re-layouts  1.42 us (6%)
  between operations  0.75 us (3%)
    pallas_call x1, Pallas kernels, body(): pl.pallas_call(edge_kernel, out_shape=(sds((rows, cols), BF16),) * 2, in_...  4.86 us
    pallas_call x1, Pallas kernels, body(): pl.pallas_call(own_kernel, out_shape=(sds((rows, cols), BF16), sds((rows,...  4.37 us
    ppermute x1, starting transfers between devices, body(): kv_o = lax.ppermute(edges((key_vectors, value_vectors), odd), AXES, across)  3.84 us
    ppermute x1, starting transfers between devices, body(): lax.ppermute(qg_o, AXES, across)  2.56 us
    ppermute x1, starting transfers between devices, body(): lax.ppermute(st_o, AXES, across)  1.96 us
    ppermute x1, starting transfers between devices, body(): lax.ppermute(qg_e, AXES, within)  1.82 us
    ppermute x1, starting transfers between devices, body(): lax.ppermute(st_e, AXES, within)  1.8 us
    pallas_call x1, Pallas kernels, body(): pl.pallas_call(local_kernel, out_shape=(sds((rows, cols), BF16), sds((sta...  1.24 us
  transfers between devices with their start and end apart: 6, of which 0 were waited for; matrix products, arithmetic and copies ran while one was open for 0% of the time, Pallas kernels for 22%

profile of v1, /device:TPU:25, one launch (start us, length us, event | category | flops | bytes accessed | tf_op | source)
XLA Modules:
  0.0 25.4 jit_solution(2072975993185858302)
XLA Ops:
  0.6 1.1 %constant_dynamic-slice_fusion = (bf16[64,1024]{1,0:T(8,128)(2,1)S(1)}, bf16[64,1024]{1,0:T(8,128)(2,1)S(1)}, bf16[64,1024]{1,0:T(8,128)(2,1)S(1)}, bf16[64,1024]{1,0:T(8,128)(2,1)S(1)}) fusion(bf16[128,1024]{1,0:T(8,128)(2,1)} %v_ref.5, s32[]{:T(128)S(6)} %select_n.9, s32[]{:T(128)S(6)} %select_n.8, bf16[128,1024]{1,0:T(8,128)(2,1)} %k_ref.5), kind=kLoop, calls=%fused_computation.2 | loop fusion | bytes 1048584 | tf_op jit(solution)/shard_map/dynamic_slice | solution.py:190
  1.8 0.0 copy-start.2
  1.8 0.0 copy-start.3
  1.8 0.0 copy-start.4
  1.8 3.8 %collective-permute-start = (bf16[128,1024]{1,0:T(8,128)(2,1)S(1)}, bf16[128,1024]{1,0:T(8,128)(2,1)S(1)}, u32[]{:S(2)}, u32[]{:S(2)}) collective-permute-start(bf16[128,1024]{1,0:T(8,128)(2,1)S(1)} %pad_maximum_fusion), channel_id=1, source_target_pairs={{1,2},{2,1},{3,4},{4,3},{5,6},{6,5},{7,8},{8,7},{9,10},{10,9},{11,... | collective-permute-start | bytes 786440 | tf_op jit(solution)/shard_map/ppermute | solution.py:192
  5.7 0.0 copy-start
  5.7 0.0 copy-start.1
  5.7 0.7 %collective-permute-start.1 = (bf16[128,1024]{1,0:T(8,128)(2,1)S(1)}, bf16[128,1024]{1,0:T(8,128)(2,1)S(1)}, u32[]{:S(2)}, u32[]{:S(2)}) collective-permute-start(bf16[128,1024]{1,0:T(8,128)(2,1)S(1)} %pad_maximum_fusion.1), channel_id=1, source_target_pairs={{0,1},{1,0},{2,3},{3,2},{4,5},{5,4},{6,7},{7,6},{8,9},{9,8},{10,11... | collective-permute-start | bytes 786440 | tf_op jit(solution)/shard_map/ppermute | solution.py:193
  6.5 0.0 copy-done.2
  6.5 0.0 copy-done.3
  6.5 0.0 copy-done.4
  6.5 0.2 copy-done
  6.6 0.1 copy-done.1
  6.7 1.2 %shard_map.77 = (bf16[128,1024]{1,0:T(8,128)(2,1)S(1)}, f32[24,128]{1,0:T(8,128)S(1)}, bf16[128,1024]{1,0:T(8,128)(2,1)S(1)}, f32[24,128]{1,0:T(8,128)S(1)}) custom-call(s32[4]{0:T(128)S(1)} %copy-done.4, bf16[128,1024]{1,0:T(8,128)(2,1)S(1)} %copy-done.2, bf16[128,1024]{1,0:T(8,128)(2,1)S(1)} %copy-done, bf16[128,1024]{1,0:T(8,128)(2,1)S(1)} %copy-done.1, ...), custom_call_target="tpu_custom_call" | custom-call | flops 268435456 | bytes 2097152 | tf_op jit(solution)/shard_map/pallas_call | solution.py:197
  8.0 2.6 %collective-permute-start.2 = (bf16[128,1024]{1,0:T(8,128)(2,1)S(1)}, bf16[128,1024]{1,0:T(8,128)(2,1)S(1)}, u32[]{:S(2)}, u32[]{:S(2)}) collective-permute-start(bf16[128,1024]{1,0:T(8,128)(2,1)S(1)} %get-tuple-element.13), channel_id=1, source_target_pairs={{1,2},{2,1},{3,4},{4,3},{5,6},{6,5},{7,8},{8,7},{9,10},{10,9},{11,... | collective-permute-start | bytes 786440 | tf_op jit(solution)/shard_map/ppermute | solution.py:205
  10.5 1.8 %collective-permute-start.4 = (bf16[128,1024]{1,0:T(8,128)(2,1)S(1)}, bf16[128,1024]{1,0:T(8,128)(2,1)S(1)}, u32[]{:S(2)}, u32[]{:S(2)}) collective-permute-start(bf16[128,1024]{1,0:T(8,128)(2,1)S(1)} %get-tuple-element.15), channel_id=1, source_target_pairs={{0,1},{1,0},{2,3},{3,2},{4,5},{5,4},{6,7},{7,6},{8,9},{9,8},{10,11... | collective-permute-start | bytes 786440 | tf_op jit(solution)/shard_map/ppermute | solution.py:206
  12.4 2.0 %collective-permute-start.3 = (f32[24,128]{1,0:T(8,128)S(1)}, f32[24,128]{1,0:T(8,128)S(1)}, u32[]{:S(2)}, u32[]{:S(2)}) collective-permute-start(f32[24,128]{1,0:T(8,128)S(1)} %get-tuple-element.14), channel_id=1, source_target_pairs={{1,2},{2,1},{3,4},{4,3},{5,6},{6,5},{7,8},{8,7},{9,10},{10,9},{11,... | collective-permute-start | bytes 36872 | tf_op jit(solution)/shard_map/ppermute | solution.py:205
  14.3 0.0 collective-permute-done.kv_o
  14.3 1.8 %collective-permute-start.5 = (f32[24,128]{1,0:T(8,128)S(1)}, f32[24,128]{1,0:T(8,128)S(1)}, u32[]{:S(2)}, u32[]{:S(2)}) collective-permute-start(f32[24,128]{1,0:T(8,128)S(1)} %get-tuple-element.16), channel_id=1, source_target_pairs={{0,1},{1,0},{2,3},{3,2},{4,5},{5,4},{6,7},{7,6},{8,9},{9,8},{10,11... | collective-permute-start | bytes 36872 | tf_op jit(solution)/shard_map/ppermute | solution.py:206
  16.1 0.0 collective-permute-done.1.kv_e
  16.1 4.4 %shard_map.76 = (bf16[128,1024]{1,0:T(8,128)(2,1)}, f32[128,1024]{1,0:T(8,128)S(1)}, f32[128,1024]{1,0:T(8,128)S(1)}) custom-call(s32[4]{0:T(128)S(1)} %copy-done.4, bf16[128,1024]{1,0:T(8,128)(2,1)S(1)} %copy-done.2, bf16[128,1024]{1,0:T(8,128)(2,1)S(1)} %copy-done, bf16[128,1024]{1,0:T(8,128)(2,1)S(1)} %copy-done.1, bf16[128,1024]{1,0:T(8,128)(2,1)S(1)} %copy-done.3, ...), custom_call_target="tpu_custom_call" | custom-call | flops 1073741824 | bytes 4194304 | tf_op jit(solution)/shard_map/pallas_call | solution.py:207
  20.5 0.0 collective-permute-done.3.st_o
  20.5 0.0 collective-permute-done.5.st_e
  20.5 0.0 collective-permute-done.2.qg_o
  20.5 0.0 collective-permute-done.4.qg_e
  20.5 4.9 %shard_map.78 = (bf16[128,1024]{1,0:T(8,128)(2,1)}, bf16[128,1024]{1,0:T(8,128)(2,1)}) custom-call(s32[4]{0:T(128)S(1)} %copy-done.4, bf16[128,1024]{1,0:T(8,128)(2,1)S(1)} %copy-done, bf16[128,1024]{1,0:T(8,128)(2,1)S(1)} %copy-done.1, bf16[128,1024]{1,0:T(8,128)(2,1)S(1)} %collective-permute-done.2.qg_o, f32[24,128]{1,0:T(8,128)S(1)} %collective-permute-done.3.st_o, ...), custom_call_target="tpu_custom_call" | custom-call | flops 134217728 | bytes 2097152 | tf_op jit(solution)/shard_map/pallas_call | solution.py:216
  (2 shorter events, 0.0 us)
Async XLA Ops:
  1.8 4.7 %copy-start.2 = (bf16[128,1024]{1,0:T(8,128)(2,1)S(1)}, bf16[128,1024]{1,0:T(8,128)(2,1)}, u32[]{:S(2)}) copy-start(bf16[128,1024]{1,0:T(8,128)(2,1)} %q_ref.3) | copy-start | bytes 786436
  1.8 4.7 %copy-start.3 = (bf16[128,1024]{1,0:T(8,128)(2,1)S(1)}, bf16[128,1024]{1,0:T(8,128)(2,1)}, u32[]{:S(2)}) copy-start(bf16[128,1024]{1,0:T(8,128)(2,1)} %g_ref.3) | copy-start | bytes 786436
  1.8 4.7 %copy-start.4 = (s32[4]{0:T(128)S(1)}, s32[4]{0:T(128)}, u32[]{:S(2)}) copy-start(s32[4]{0:T(128)} %len_ref.5) | copy-start | bytes 52
  1.8 12.5 %collective-permute-start = (bf16[128,1024]{1,0:T(8,128)(2,1)S(1)}, bf16[128,1024]{1,0:T(8,128)(2,1)S(1)}, u32[]{:S(2)}, u32[]{:S(2)}) collective-permute-start(bf16[128,1024]{1,0:T(8,128)(2,1)S(1)} %pad_maximum_fusion), channel_id=1, source_target_pairs={{1,2},{2,1},{3,4},{4,3},{5,6},{6,5},{7,8},{8,7},{9,10},{10,9},{11,... | collective-permute-start | bytes 786440 | tf_op jit(solution)/shard_map/ppermute | solution.py:192
  5.7 1.0 %copy-start = (bf16[128,1024]{1,0:T(8,128)(2,1)S(1)}, bf16[128,1024]{1,0:T(8,128)(2,1)}, u32[]{:S(2)}) copy-start(bf16[128,1024]{1,0:T(8,128)(2,1)} %k_ref.5) | copy-start | bytes 786436
  5.7 1.0 %copy-start.1 = (bf16[128,1024]{1,0:T(8,128)(2,1)S(1)}, bf16[128,1024]{1,0:T(8,128)(2,1)}, u32[]{:S(2)}) copy-start(bf16[128,1024]{1,0:T(8,128)(2,1)} %v_ref.5) | copy-start | bytes 786436
  5.7 10.4 %collective-permute-start.1 = (bf16[128,1024]{1,0:T(8,128)(2,1)S(1)}, bf16[128,1024]{1,0:T(8,128)(2,1)S(1)}, u32[]{:S(2)}, u32[]{:S(2)}) collective-permute-start(bf16[128,1024]{1,0:T(8,128)(2,1)S(1)} %pad_maximum_fusion.1), channel_id=1, source_target_pairs={{0,1},{1,0},{2,3},{3,2},{4,5},{5,4},{6,7},{7,6},{8,9},{9,8},{10,11... | collective-permute-start | bytes 786440 | tf_op jit(solution)/shard_map/ppermute | solution.py:193
  8.0 12.6 %collective-permute-start.2 = (bf16[128,1024]{1,0:T(8,128)(2,1)S(1)}, bf16[128,1024]{1,0:T(8,128)(2,1)S(1)}, u32[]{:S(2)}, u32[]{:S(2)}) collective-permute-start(bf16[128,1024]{1,0:T(8,128)(2,1)S(1)} %get-tuple-element.13), channel_id=1, source_target_pairs={{1,2},{2,1},{3,4},{4,3},{5,6},{6,5},{7,8},{8,7},{9,10},{10,9},{11,... | collective-permute-start | bytes 786440 | tf_op jit(solution)/shard_map/ppermute | solution.py:205
  10.5 10.0 %collective-permute-start.4 = (bf16[128,1024]{1,0:T(8,128)(2,1)S(1)}, bf16[128,1024]{1,0:T(8,128)(2,1)S(1)}, u32[]{:S(2)}, u32[]{:S(2)}) collective-permute-start(bf16[128,1024]{1,0:T(8,128)(2,1)S(1)} %get-tuple-element.15), channel_id=1, source_target_pairs={{0,1},{1,0},{2,3},{3,2},{4,5},{5,4},{6,7},{7,6},{8,9},{9,8},{10,11... | collective-permute-start | bytes 786440 | tf_op jit(solution)/shard_map/ppermute | solution.py:206
  12.4 8.2 %collective-permute-start.3 = (f32[24,128]{1,0:T(8,128)S(1)}, f32[24,128]{1,0:T(8,128)S(1)}, u32[]{:S(2)}, u32[]{:S(2)}) collective-permute-start(f32[24,128]{1,0:T(8,128)S(1)} %get-tuple-element.14), channel_id=1, source_target_pairs={{1,2},{2,1},{3,4},{4,3},{5,6},{6,5},{7,8},{8,7},{9,10},{10,9},{11,... | collective-permute-start | bytes 36872 | tf_op jit(solution)/shard_map/ppermute | solution.py:205
  14.3 6.2 %collective-permute-start.5 = (f32[24,128]{1,0:T(8,128)S(1)}, f32[24,128]{1,0:T(8,128)S(1)}, u32[]{:S(2)}, u32[]{:S(2)}) collective-permute-start(f32[24,128]{1,0:T(8,128)S(1)} %get-tuple-element.16), channel_id=1, source_target_pairs={{0,1},{1,0},{2,3},{3,2},{4,5},{5,4},{6,7},{7,6},{8,9},{9,8},{10,11... | collective-permute-start | bytes 36872 | tf_op jit(solution)/shard_map/ppermute | solution.py:206

commit v2 on v1

v2 whole, which is shorter than its diff:
```python
import jax
import jax.numpy as jnp
from jax import lax
from jax.experimental import pallas as pl
from jax.experimental.pallas import tpu as pltpu
from jax.sharding import PartitionSpec as P

DH = 64
WIN = 64
PAIR = 2 * DH
STATS = 8
SCALE = DH ** (-0.5)
NEG = -1e30
AXES = ("blk", "head")
F32 = jnp.float32
BF16 = jnp.bfloat16


def flat_index():
    return lax.axis_index("blk") * lax.axis_size("head") + lax.axis_index("head")


def recording_of(pos, len_ref):
    rec = jnp.where(pos < 0, -1, 0)
    end = jnp.int32(0)
    for r in range(len_ref.shape[0]):
        end = end + len_ref[r]
        rec = rec + jnp.where(pos >= end, 1, 0)
    return rec


def bias_of(key_first, query_first, keys, queries, lane_queries, len_ref):
    kpos = key_first + lax.broadcasted_iota(jnp.int32, (keys, 1), 0)
    qpos = query_first + lax.broadcasted_iota(jnp.int32, (1, queries), 1) % lane_queries
    near = jnp.abs(kpos - qpos) <= WIN
    same = recording_of(kpos, len_ref) == recording_of(qpos, len_ref)
    return jnp.where(near & same, 0.0, NEG).astype(F32)


def split_heads(pair):
    lane = lax.broadcasted_iota(jnp.int32, pair.shape, 1)
    zero = jnp.zeros_like(pair)
    return jnp.concatenate([jnp.where(lane < DH, pair, zero), jnp.where(lane < DH, zero, pair)], axis=0)


def nt(a, b):
    return lax.dot_general(a, b, (((1,), (1,)), ((), ())), preferred_element_type=F32)


def nn(a, b):
    return lax.dot_general(a, b, (((1,), (0,)), ((), ())), preferred_element_type=F32)


def tn(a, b):
    return lax.dot_general(a, b, (((0,), (0,)), ((), ())), preferred_element_type=F32)


def pieces(x):
    hi = x.astype(BF16).astype(F32)
    mid = (x - hi).astype(BF16).astype(F32)
    return [hi, mid, x - hi - mid]


def local_kernel(len_ref, q_ref, k_ref, v_ref, g_ref, qs_o, qs_e, own_bias, bias_o, bias_e):
    rows, cols = q_ref.shape
    me = flat_index()
    odd = lax.rem(me, 2)
    base = me * rows
    half = rows // 2
    for out, side in ((qs_o, odd), (qs_e, 1 - odd)):
        first = pl.multiple_of(side * half, half)
        out[:half, :] = q_ref[pl.ds(first, half), :] * BF16(SCALE)
        out[half:rows, :] = g_ref[pl.ds(first, half), :]
    own_bias[...] = bias_of(base - half, base, 2 * rows, rows, rows, len_ref)
    for out, side in ((bias_o, odd), (bias_e, 1 - odd)):
        out[...] = bias_of(base + side * half, base + jnp.where(side == 1, rows, -half), half, rows, half, len_ref)
    bias = own_bias[half : half + rows]
    bias = jnp.concatenate([bias, bias], axis=1)
    lane = lax.broadcasted_iota(jnp.int32, (1, rows), 1)
    for p in range(cols // PAIR):
        cs = slice(p * PAIR, (p + 1) * PAIR)
        qq = split_heads(q_ref[:, cs]) * BF16(SCALE)
        gg = split_heads(g_ref[:, cs])
        s = nt(k_ref[:, cs], qq) + bias
        dp = nt(v_ref[:, cs], gg)
        m = jnp.max(s, axis=0, keepdims=True).astype(BF16).astype(F32)
        e = jnp.exp(s - m)
        l = jnp.sum(e, axis=0, keepdims=True)
        d = jnp.sum(e * dp, axis=0, keepdims=True)
        stat = jnp.concatenate([m] + pieces(l) + pieces(d) + [jnp.zeros_like(m)], axis=0)
        a, b = stat[:, :rows], stat[:, rows:]
        lo = jnp.where(lane < half, a, pltpu.roll(b, half, 1))
        hi = jnp.where(lane < half, pltpu.roll(a, half, 1), b)
        qs_o[rows:, cs] = jnp.where(odd == 1, hi, lo).astype(BF16)
        qs_e[rows:, cs] = jnp.where(odd == 1, lo, hi).astype(BF16)


def own_kernel(bias_ref, q_ref, k_ref, v_ref, g_ref, kv_o, kv_e, dq_ref, dk_ref, dv_ref, kx, vx):
    rows, cols = q_ref.shape
    odd = lax.rem(flat_index(), 2)
    half = rows // 2
    for dst, own, o in ((kx, k_ref, 0), (vx, v_ref, half)):
        dst[half : half + rows, :] = own[...]

        @pl.when(odd == 1)
        def _():
            dst[:half, :] = kv_e[o : o + half, :]
            dst[half + rows :, :] = kv_o[o : o + half, :]

        @pl.when(odd == 0)
        def _():
            dst[:half, :] = kv_o[o : o + half, :]
            dst[half + rows :, :] = kv_e[o : o + half, :]

    bias = jnp.concatenate([bias_ref[...], bias_ref[...]], axis=1)
    lane = lax.broadcasted_iota(jnp.int32, (rows, PAIR), 1)
    for p in range(cols // PAIR):
        cs = slice(p * PAIR, (p + 1) * PAIR)
        qq = split_heads(q_ref[:, cs]) * BF16(SCALE)
        gg = split_heads(g_ref[:, cs])
        kp = kx[:, cs]
        s = nt(kp, qq) + bias
        dp = nt(vx[:, cs], gg)
        m = jnp.max(s, axis=0, keepdims=True)
        e = jnp.exp(s - m)
        inv = 1.0 / jnp.sum(e, axis=0, keepdims=True)
        prob = e * inv
        delta = jnp.sum(prob * dp, axis=0, keepdims=True)
        ds = (prob * (dp - delta)).astype(BF16)
        dv_ref[:, cs] = nn(prob[half : half + rows].astype(BF16), gg)
        dk_ref[:, cs] = nn(ds[half : half + rows], qq)
        dq2 = tn(ds, kp)
        dq_ref[:, cs] = (jnp.where(lane < DH, dq2[:rows], dq2[rows:]) * SCALE).astype(BF16)


def edge_kernel(bias_o, bias_e, k_ref, v_ref, qs_o, qs_e, dka_ref, dva_ref, dk_ref, dv_ref):
    rows, cols = k_ref.shape
    odd = lax.rem(flat_index(), 2)
    half = rows // 2
    sides = []
    for qs, bias, side in ((qs_o, bias_o, odd), (qs_e, bias_e, 1 - odd)):
        sides.append((qs, bias[...], pl.ds(pl.multiple_of(side * half, half), half)))
    items = [(slice(p * PAIR, (p + 1) * PAIR),) + side for p in range(cols // PAIR) for side in sides]
    scored = []
    for cs, qs, bias, rs in items:
        qq, gg = split_heads(qs[:half, cs]), split_heads(qs[half:rows, cs])
        scored.append((qq, gg, nt(k_ref[rs, cs], qq), nt(v_ref[rs, cs], gg)))
    graded = []
    for (cs, qs, bias, rs), (qq, gg, s, dp) in zip(items, scored):
        stat = qs[rows:, cs].astype(F32)
        m0 = stat[0:1]
        l0 = stat[1:2] + stat[2:3] + stat[3:4]
        d0 = stat[4:5] + stat[5:6] + stat[6:7]
        s = s + bias
        m = jnp.maximum(m0, jnp.max(s, axis=0, keepdims=True))
        e = jnp.exp(s - m)
        a = jnp.exp(m0 - m)
        l = a * l0 + jnp.sum(e, axis=0, keepdims=True)
        d = a * d0 + jnp.sum(e * dp, axis=0, keepdims=True)
        inv = 1.0 / jnp.where(l > 0, l, 1.0)
        prob = e * inv
        graded.append((qq, gg, prob.astype(BF16), (prob * (dp - d * inv)).astype(BF16)))
    for (cs, qs, bias, rs), (qq, gg, prob, ds) in zip(items, graded):
        dv_ref[rs, cs] = (dva_ref[rs, cs] + nn(prob, gg)).astype(BF16)
        dk_ref[rs, cs] = (dka_ref[rs, cs] + nn(ds, qq)).astype(BF16)


VM = pl.BlockSpec(memory_space=pltpu.VMEM)
SM = pl.BlockSpec(memory_space=pltpu.SMEM)


def body(queries, key_vectors, value_vectors, grad_output, lengths):
    rows, cols = queries.shape
    half = rows // 2
    count = lax.axis_size("blk") * lax.axis_size("head")
    odd = lax.rem(flat_index(), 2)
    across = [(a, b) for i in range(1, count - 1, 2) for a, b in ((i, i + 1), (i + 1, i))]
    within = [(a, b) for i in range(0, count, 2) for a, b in ((i, i + 1), (i + 1, i))]

    def edges(arrays, side):
        return jnp.concatenate([lax.dynamic_slice_in_dim(x, side * half, half, 0) for x in arrays], axis=0)

    kv_o = lax.ppermute(edges((key_vectors, value_vectors), odd), AXES, across)
    kv_e = lax.ppermute(edges((key_vectors, value_vectors), 1 - odd), AXES, within)
    sds = jax.ShapeDtypeStruct
    params = pltpu.CompilerParams(vmem_limit_bytes=20 << 20)
    sent, edge = sds((rows + STATS, cols), BF16), sds((half, rows), F32)
    qs_o, qs_e, own_bias, bias_o, bias_e = pl.pallas_call(
        local_kernel,
        out_shape=(sent, sent, sds((2 * rows, rows), F32), edge, edge),
        in_specs=[SM] + [VM] * 4,
        out_specs=(VM,) * 5,
        compiler_params=params,
        cost_estimate=pl.CostEstimate(flops=1 << 28, bytes_accessed=2 << 20, transcendentals=1 << 18),
    )(lengths, queries, key_vectors, value_vectors, grad_output)
    qs_o = lax.ppermute(qs_o, AXES, across)
    qs_e = lax.ppermute(qs_e, AXES, within)
    dq, dk, dv = pl.pallas_call(
        own_kernel,
        out_shape=(sds((rows, cols), BF16), sds((rows, cols), F32), sds((rows, cols), F32)),
        in_specs=[VM] * 7,
        out_specs=(VM,) * 3,
        scratch_shapes=[pltpu.VMEM((2 * rows, cols), BF16)] * 2,
        compiler_params=params,
        cost_estimate=pl.CostEstimate(flops=1 << 30, bytes_accessed=4 << 20, transcendentals=1 << 19),
    )(own_bias, queries, key_vectors, value_vectors, grad_output, kv_o, kv_e)
    dk, dv = pl.pallas_call(
        edge_kernel,
        out_shape=(sds((rows, cols), BF16),) * 2,
        in_specs=[VM] * 8,
        out_specs=(VM,) * 2,
        compiler_params=params,
        cost_estimate=pl.CostEstimate(flops=1 << 27, bytes_accessed=2 << 20, transcendentals=1 << 17),
    )(bias_o, bias_e, key_vectors, value_vectors, qs_o, qs_e, dk, dv)
    return dq, dk, dv


def solution(mesh):
    return jax.shard_map(
        body,
        mesh=mesh,
        in_specs=(P(AXES, None),) * 4 + (P(),),
        out_specs=(P(AXES, None),) * 3,
        check_vma=False,
    )
```

time: 25.6 us -> 21.1 us (0.82)
  starting transfers between devices: 12.7 us -> 8.94 us
  Pallas kernels: 10.5 us -> 7.17 us
  waiting for transfers between devices: 0.02 us -> 2.63 us
    ppermute x4 -> x2, starting transfers between devices: 8.15 us -> 4.39 us  [the longest x1 2.56 us: body(): qs_o = lax.ppermute(qs_o, AXES, across)]
    pallas_call x1, Pallas kernels: 4.86 us -> 1.96 us  [body(): pl.pallas_call(edge_kernel, out_shape=(sds((rows, cols), BF16),) * 2, in_...]
    ppermute x4 -> x2, waiting for transfers between devices: 0.01 us -> 2.6 us  [the longest x1 2.59 us: body(): qs_o = lax.ppermute(qs_o, AXES, across)]
    pallas_call x1, Pallas kernels: 4.37 us -> 3.82 us  [body(): pl.pallas_call(own_kernel, out_shape=(sds((rows, cols), BF16), sds((rows,...]
  transfers between devices with their start and end apart: 6 -> 4, of which waited for: 0 -> 1; matrix products, arithmetic and copies ran while one was open for 0% -> 0% of each run, Pallas kernels for 22% -> 25%
where the time goes in v2:
time: 21.1 us; the launch traced here: 20.9 us
  starting transfers between devices  8.94 us (42%)
  Pallas kernels  7.17 us (34%)
  waiting for transfers between devices  2.63 us (12%)
  local copies, waits for them, and re-layouts  1.42 us (7%)
  between operations  0.72 us (3%)
    ppermute x1, starting transfers between devices, body(): kv_o = lax.ppermute(edges((key_vectors, value_vectors), odd), AXES, across)  3.84 us
    pallas_call x1, Pallas kernels, body(): pl.pallas_call(own_kernel, out_shape=(sds((rows, cols), BF16), sds((rows,...  3.82 us
    ppermute x1, waiting for transfers between devices, body(): qs_o = lax.ppermute(qs_o, AXES, across)  2.59 us
    ppermute x1, starting transfers between devices, body(): qs_o = lax.ppermute(qs_o, AXES, across)  2.56 us
    pallas_call x1, Pallas kernels, body(): pl.pallas_call(edge_kernel, out_shape=(sds((rows, cols), BF16),) * 2, in_...  1.96 us
    ppermute x1, starting transfers between devices, body(): qs_e = lax.ppermute(qs_e, AXES, within)  1.83 us
    pallas_call x1, Pallas kernels, body(): pl.pallas_call(local_kernel, out_shape=(sent, sent, sds((2 * rows, rows),...  1.39 us
    dynamic_slice x1, local copies, waits for them, and re-layouts, edges(): lax.dynamic_slice_in_dim(x, side * half, half, 0)  1.14 us
  transfers between devices with their start and end apart: 4, of which 1 were waited for; matrix products, arithmetic and copies ran while one was open for 0% of the time, Pallas kernels for 25%

profile of v2, /device:TPU:25, one launch (start us, length us, event | category | flops | bytes accessed | tf_op | source)
XLA Modules:
  0.0 20.9 jit_solution(15469592134258036073)
XLA Ops:
  0.6 1.1 %constant_dynamic-slice_fusion = (bf16[64,1024]{1,0:T(8,128)(2,1)S(1)}, bf16[64,1024]{1,0:T(8,128)(2,1)S(1)}, bf16[64,1024]{1,0:T(8,128)(2,1)S(1)}, bf16[64,1024]{1,0:T(8,128)(2,1)S(1)}) fusion(bf16[128,1024]{1,0:T(8,128)(2,1)} %v_ref.5, s32[]{:T(128)S(6)} %select_n.9, s32[]{:T(128)S(6)} %select_n.8, bf16[128,1024]{1,0:T(8,128)(2,1)} %k_ref.5), kind=kLoop, calls=%fused_computation.2 | loop fusion | bytes 1048584 | tf_op jit(solution)/shard_map/dynamic_slice | solution.py:181
  1.8 0.0 copy-start.2
  1.8 0.0 copy-start.3
  1.8 0.0 copy-start.4
  1.8 3.8 %collective-permute-start = (bf16[128,1024]{1,0:T(8,128)(2,1)S(1)}, bf16[128,1024]{1,0:T(8,128)(2,1)S(1)}, u32[]{:S(2)}, u32[]{:S(2)}) collective-permute-start(bf16[128,1024]{1,0:T(8,128)(2,1)S(1)} %pad_maximum_fusion), channel_id=1, source_target_pairs={{1,2},{2,1},{3,4},{4,3},{5,6},{6,5},{7,8},{8,7},{9,10},{10,9},{11,... | collective-permute-start | bytes 786440 | tf_op jit(solution)/shard_map/ppermute | solution.py:183
  5.7 0.0 copy-start
  5.7 0.0 copy-start.1
  5.7 0.7 %collective-permute-start.1 = (bf16[128,1024]{1,0:T(8,128)(2,1)S(1)}, bf16[128,1024]{1,0:T(8,128)(2,1)S(1)}, u32[]{:S(2)}, u32[]{:S(2)}) collective-permute-start(bf16[128,1024]{1,0:T(8,128)(2,1)S(1)} %pad_maximum_fusion.1), channel_id=1, source_target_pairs={{0,1},{1,0},{2,3},{3,2},{4,5},{5,4},{6,7},{7,6},{8,9},{9,8},{10,11... | collective-permute-start | bytes 786440 | tf_op jit(solution)/shard_map/ppermute | solution.py:184
  6.5 0.0 copy-done.2
  6.5 0.0 copy-done.3
  6.5 0.0 copy-done.4
  6.5 0.2 copy-done
  6.6 0.1 copy-done.1
  6.7 1.4 %shard_map.76 = (bf16[136,1024]{1,0:T(8,128)(2,1)S(1)}, bf16[136,1024]{1,0:T(8,128)(2,1)S(1)}, f32[256,128]{1,0:T(8,128)S(1)}, f32[64,128]{1,0:T(8,128)S(1)}, f32[64,128]{1,0:T(8,128)S(1)}) custom-call(s32[4]{0:T(128)S(1)} %copy-done.4, bf16[128,1024]{1,0:T(8,128)(2,1)S(1)} %copy-done.2, bf16[128,1024]{1,0:T(8,128)(2,1)S(1)} %copy-done, ...), custom_call_target="tpu_custom_call" | custom-call | flops 268435456 | bytes 2097152 | tf_op jit(solution)/shard_map/pallas_call | solution.py:188
  8.1 2.6 %collective-permute-start.2 = (bf16[136,1024]{1,0:T(8,128)(2,1)S(1)}, bf16[136,1024]{1,0:T(8,128)(2,1)S(1)}, u32[]{:S(2)}, u32[]{:S(2)}) collective-permute-start(bf16[136,1024]{1,0:T(8,128)(2,1)S(1)} %get-tuple-element.17), channel_id=1, source_target_pairs={{1,2},{2,1},{3,4},{4,3},{5,6},{6,5},{7,8},{8,7},{9,10},{10,9},{11,... | collective-permute-start | bytes 835592 | tf_op jit(solution)/shard_map/ppermute | solution.py:196
  10.7 1.8 %collective-permute-start.3 = (bf16[136,1024]{1,0:T(8,128)(2,1)S(1)}, bf16[136,1024]{1,0:T(8,128)(2,1)S(1)}, u32[]{:S(2)}, u32[]{:S(2)}) collective-permute-start(bf16[136,1024]{1,0:T(8,128)(2,1)S(1)} %get-tuple-element.18), channel_id=1, source_target_pairs={{0,1},{1,0},{2,3},{3,2},{4,5},{5,4},{6,7},{7,6},{8,9},{9,8},{10,11... | collective-permute-start | bytes 835592 | tf_op jit(solution)/shard_map/ppermute | solution.py:197
  12.5 0.0 collective-permute-done.kv_o
  12.5 0.0 collective-permute-done.1.kv_e
  12.5 3.8 %shard_map.77 = (bf16[128,1024]{1,0:T(8,128)(2,1)}, f32[128,1024]{1,0:T(8,128)S(1)}, f32[128,1024]{1,0:T(8,128)S(1)}) custom-call(f32[256,128]{1,0:T(8,128)S(1)} %get-tuple-element.13.bias_ref, bf16[128,1024]{1,0:T(8,128)(2,1)S(1)} %copy-done.2, bf16[128,1024]{1,0:T(8,128)(2,1)S(1)} %copy-done, bf16[128,1024]{1,0:T(8,128)(2,1)S(1)} %copy-done.1, ...), custom_call_target="tpu_custom_call" | custom-call | flops 1073741824 | bytes 4194304 | tf_op jit(solution)/shard_map/pallas_call | solution.py:198
  16.4 2.6 %collective-permute-done.2.qs_o = bf16[136,1024]{1,0:T(8,128)(2,1)S(1)} collective-permute-done((bf16[136,1024]{1,0:T(8,128)(2,1)S(1)}, bf16[136,1024]{1,0:T(8,128)(2,1)S(1)}, u32[]{:S(2)}, u32[]{:S(2)}) %collective-permute-start.2) | collective-permute-done | bytes 278560 | tf_op jit(solution)/shard_map/ppermute | solution.py:196
  19.0 0.0 collective-permute-done.3.qs_e
  19.0 2.0 %shard_map.78 = (bf16[128,1024]{1,0:T(8,128)(2,1)}, bf16[128,1024]{1,0:T(8,128)(2,1)}) custom-call(f32[64,128]{1,0:T(8,128)S(1)} %get-tuple-element.15.bias_o, f32[64,128]{1,0:T(8,128)S(1)} %get-tuple-element.16.bias_e, bf16[128,1024]{1,0:T(8,128)(2,1)S(1)} %copy-done, bf16[128,1024]{1,0:T(8,128)(2,1)S(1)} %copy-done.1, ...), custom_call_target="tpu_custom_call" | custom-call | flops 134217728 | bytes 2097152 | tf_op jit(solution)/shard_map/pallas_call | solution.py:207
  (2 shorter events, 0.0 us)
Async XLA Ops:
  1.8 4.7 %copy-start.2 = (bf16[128,1024]{1,0:T(8,128)(2,1)S(1)}, bf16[128,1024]{1,0:T(8,128)(2,1)}, u32[]{:S(2)}) copy-start(bf16[128,1024]{1,0:T(8,128)(2,1)} %q_ref.3) | copy-start | bytes 786436
  1.8 4.7 %copy-start.3 = (bf16[128,1024]{1,0:T(8,128)(2,1)S(1)}, bf16[128,1024]{1,0:T(8,128)(2,1)}, u32[]{:S(2)}) copy-start(bf16[128,1024]{1,0:T(8,128)(2,1)} %g_ref.3) | copy-start | bytes 786436
  1.8 4.7 %copy-start.4 = (s32[4]{0:T(128)S(1)}, s32[4]{0:T(128)}, u32[]{:S(2)}) copy-start(s32[4]{0:T(128)} %len_ref.1) | copy-start | bytes 52
  1.8 10.7 %collective-permute-start = (bf16[128,1024]{1,0:T(8,128)(2,1)S(1)}, bf16[128,1024]{1,0:T(8,128)(2,1)S(1)}, u32[]{:S(2)}, u32[]{:S(2)}) collective-permute-start(bf16[128,1024]{1,0:T(8,128)(2,1)S(1)} %pad_maximum_fusion), channel_id=1, source_target_pairs={{1,2},{2,1},{3,4},{4,3},{5,6},{6,5},{7,8},{8,7},{9,10},{10,9},{11,... | collective-permute-start | bytes 786440 | tf_op jit(solution)/shard_map/ppermute | solution.py:183
  5.7 1.0 %copy-start = (bf16[128,1024]{1,0:T(8,128)(2,1)S(1)}, bf16[128,1024]{1,0:T(8,128)(2,1)}, u32[]{:S(2)}) copy-start(bf16[128,1024]{1,0:T(8,128)(2,1)} %k_ref.5) | copy-start | bytes 786436
  5.7 1.0 %copy-start.1 = (bf16[128,1024]{1,0:T(8,128)(2,1)S(1)}, bf16[128,1024]{1,0:T(8,128)(2,1)}, u32[]{:S(2)}) copy-start(bf16[128,1024]{1,0:T(8,128)(2,1)} %v_ref.5) | copy-start | bytes 786436
  5.7 6.8 %collective-permute-start.1 = (bf16[128,1024]{1,0:T(8,128)(2,1)S(1)}, bf16[128,1024]{1,0:T(8,128)(2,1)S(1)}, u32[]{:S(2)}, u32[]{:S(2)}) collective-permute-start(bf16[128,1024]{1,0:T(8,128)(2,1)S(1)} %pad_maximum_fusion.1), channel_id=1, source_target_pairs={{0,1},{1,0},{2,3},{3,2},{4,5},{5,4},{6,7},{7,6},{8,9},{9,8},{10,11... | collective-permute-start | bytes 786440 | tf_op jit(solution)/shard_map/ppermute | solution.py:184
  8.1 10.8 %collective-permute-start.2 = (bf16[136,1024]{1,0:T(8,128)(2,1)S(1)}, bf16[136,1024]{1,0:T(8,128)(2,1)S(1)}, u32[]{:S(2)}, u32[]{:S(2)}) collective-permute-start(bf16[136,1024]{1,0:T(8,128)(2,1)S(1)} %get-tuple-element.17), channel_id=1, source_target_pairs={{1,2},{2,1},{3,4},{4,3},{5,6},{6,5},{7,8},{8,7},{9,10},{10,9},{11,... | collective-permute-start | bytes 835592 | tf_op jit(solution)/shard_map/ppermute | solution.py:196
  10.7 8.3 %collective-permute-start.3 = (bf16[136,1024]{1,0:T(8,128)(2,1)S(1)}, bf16[136,1024]{1,0:T(8,128)(2,1)S(1)}, u32[]{:S(2)}, u32[]{:S(2)}) collective-permute-start(bf16[136,1024]{1,0:T(8,128)(2,1)S(1)} %get-tuple-element.18), channel_id=1, source_target_pairs={{0,1},{1,0},{2,3},{3,2},{4,5},{5,4},{6,7},{7,6},{8,9},{9,8},{10,11... | collective-permute-start | bytes 835592 | tf_op jit(solution)/shard_map/ppermute | solution.py:197

commit v3 on v2

v3 whole, which is shorter than its diff:
```python
import functools

import jax
import jax.numpy as jnp
from jax import lax
from jax.experimental import pallas as pl
from jax.experimental.pallas import tpu as pltpu
from jax.sharding import PartitionSpec as P

DH = 64
WIN = 64
PAIR = 2 * DH
STATS = 8
OWN_GROUP = 8
SCALE = DH ** (-0.5)
NEG = -1e30
AXES = ("blk", "head")
F32 = jnp.float32
BF16 = jnp.bfloat16


def flat_index():
    return lax.axis_index("blk") * lax.axis_size("head") + lax.axis_index("head")


def recording_of(pos, len_ref):
    rec = jnp.where(pos < 0, -1, 0)
    end = jnp.int32(0)
    for r in range(len_ref.shape[0]):
        end = end + len_ref[r]
        rec = rec + jnp.where(pos >= end, 1, 0)
    return rec


def bias_of(key_first, query_first, keys, queries, lane_queries, len_ref):
    kpos = key_first + lax.broadcasted_iota(jnp.int32, (keys, 1), 0)
    qpos = query_first + lax.broadcasted_iota(jnp.int32, (1, queries), 1) % lane_queries
    near = jnp.abs(kpos - qpos) <= WIN
    same = recording_of(kpos, len_ref) == recording_of(qpos, len_ref)
    return jnp.where(near & same, 0.0, NEG).astype(F32)


def split_heads(pair):
    lane = lax.broadcasted_iota(jnp.int32, pair.shape, 1)
    zero = jnp.zeros_like(pair)
    return jnp.concatenate([jnp.where(lane < DH, pair, zero), jnp.where(lane < DH, zero, pair)], axis=0)


def nt(a, b):
    return lax.dot_general(a, b, (((1,), (1,)), ((), ())), preferred_element_type=F32)


def nn(a, b):
    return lax.dot_general(a, b, (((1,), (0,)), ((), ())), preferred_element_type=F32)


def tn(a, b):
    return lax.dot_general(a, b, (((0,), (0,)), ((), ())), preferred_element_type=F32)


def pieces(x):
    hi = x.astype(BF16).astype(F32)
    mid = (x - hi).astype(BF16).astype(F32)
    return [hi, mid, x - hi - mid]


def prep_kernel(len_hbm, k_hbm, v_hbm, k_ref, v_ref, kv_o, k_e, v_e, own_bias, bias_o, bias_e, len_ref, sems):
    copies = [
        pltpu.make_async_copy(len_hbm, len_ref, sems.at[0]),
        pltpu.make_async_copy(k_hbm, k_ref, sems.at[1]),
        pltpu.make_async_copy(v_hbm, v_ref, sems.at[2]),
    ]
    for copy in copies:
        copy.start()
    rows = k_ref.shape[0]
    half = rows // 2
    me = flat_index()
    odd = lax.rem(me, 2)
    base = me * rows
    copies[0].wait()
    own_bias[...] = bias_of(base, base, rows, rows, rows, len_ref)
    for out, side in ((bias_o, odd), (bias_e, 1 - odd)):
        mine, other = base + side * half, base + jnp.where(side == 1, rows, -half)
        out[:rows, :] = bias_of(base, mine, rows, rows, half, len_ref)
        out[rows : rows + half, :] = bias_of(other, mine, half, rows, half, len_ref)
        out[rows + half :, :] = bias_of(mine, other, half, rows, half, len_ref)
    for n, (ref, out) in enumerate(((k_ref, k_e), (v_ref, v_e))):
        copies[n + 1].wait()
        kv_o[n * half : (n + 1) * half, :] = ref[pl.ds(pl.multiple_of(odd * half, half), half), :]
        out[...] = ref[pl.ds(pl.multiple_of((1 - odd) * half, half), half), :]


def local_kernel(bias_ref, q_ref, k_ref, v_ref, g_ref, qs_o, q_e, gs_e):
    rows, cols = q_ref.shape
    odd = lax.rem(flat_index(), 2)
    half = rows // 2
    first, other = pl.multiple_of(odd * half, half), pl.multiple_of((1 - odd) * half, half)
    qs_o[:half, :] = q_ref[pl.ds(first, half), :] * BF16(SCALE)
    qs_o[half:rows, :] = g_ref[pl.ds(first, half), :]
    q_e[...] = q_ref[pl.ds(other, half), :] * BF16(SCALE)
    gs_e[:half, :] = g_ref[pl.ds(other, half), :]
    bias = bias_ref[...]
    bias = jnp.concatenate([bias, bias], axis=1)
    lane = lax.broadcasted_iota(jnp.int32, (1, rows), 1)
    for p in range(cols // PAIR):
        cs = slice(p * PAIR, (p + 1) * PAIR)
        qq = split_heads(q_ref[:, cs]) * BF16(SCALE)
        gg = split_heads(g_ref[:, cs])
        s = nt(k_ref[:, cs], qq) + bias
        dp = nt(v_ref[:, cs], gg)
        m = jnp.max(s, axis=0, keepdims=True).astype(BF16).astype(F32)
        e = jnp.exp(s - m)
        l = jnp.sum(e, axis=0, keepdims=True)
        d = jnp.sum(e * dp, axis=0, keepdims=True)
        stat = jnp.concatenate([m] + pieces(l) + pieces(d) + [jnp.zeros_like(m)], axis=0)
        a, b = stat[:, :rows], stat[:, rows:]
        lo = jnp.where(lane < half, a, pltpu.roll(b, half, 1))
        hi = jnp.where(lane < half, pltpu.roll(a, half, 1), b)
        qs_o[rows:, cs] = jnp.where(odd == 1, hi, lo).astype(BF16)
        gs_e[half:, cs] = jnp.where(odd == 1, lo, hi).astype(BF16)


def side_rows(across, half):
    odd = lax.rem(flat_index(), 2)
    return pl.ds(pl.multiple_of((odd if across else 1 - odd) * half, half), half)


def own_half(rs, group, bias_ref, q_ref, k_ref, v_ref, g_ref, kn_ref, vn_ref, dq_ref, add):
    rows = k_ref.shape[0]
    half = rows // 2
    lane = lax.broadcasted_iota(jnp.int32, (half, PAIR), 1)
    near, far = bias_ref[:rows, :], bias_ref[rows : rows + half, :]
    scored = []
    for cs in group:
        qq = split_heads(q_ref[rs, cs]) * BF16(SCALE)
        gg = split_heads(g_ref[rs, cs])
        s = nt(k_ref[:, cs], qq), nt(kn_ref[:, cs], qq)
        dp = nt(v_ref[:, cs], gg), nt(vn_ref[:, cs], gg)
        scored.append((qq, gg, s, dp))
    graded = []
    for qq, gg, s, dp in scored:
        s = s[0] + near, s[1] + far
        m = jnp.maximum(jnp.max(s[0], axis=0, keepdims=True), jnp.max(s[1], axis=0, keepdims=True))
        e = [jnp.exp(x - m) for x in s]
        inv = 1.0 / (jnp.sum(e[0], axis=0, keepdims=True) + jnp.sum(e[1], axis=0, keepdims=True))
        prob = [x * inv for x in e]
        delta = jnp.sum(prob[0] * dp[0], axis=0, keepdims=True) + jnp.sum(prob[1] * dp[1], axis=0, keepdims=True)
        ds = [(x * (y - delta)).astype(BF16) for x, y in zip(prob, dp)]
        graded.append((qq, gg, prob[0].astype(BF16), ds))
    for cs, (qq, gg, prob, ds) in zip(group, graded):
        add(cs, nn(ds[0], qq), nn(prob, gg))
        dq2 = tn(ds[0], k_ref[:, cs]) + tn(ds[1], kn_ref[:, cs])
        dq_ref[:, cs] = (jnp.where(lane < DH, dq2[:half], dq2[half:]) * SCALE).astype(BF16)


def edge(rs, group, bias_ref, k_ref, v_ref, qn_ref, gs_ref, add):
    rows = k_ref.shape[0]
    half = rows // 2
    bias = bias_ref[rows + half :, :]
    scored = []
    for cs in group:
        qq, gg = split_heads(qn_ref[:, cs]), split_heads(gs_ref[:half, cs])
        scored.append((qq, gg, nt(k_ref[rs, cs], qq), nt(v_ref[rs, cs], gg)))
    graded = []
    for cs, (qq, gg, s, dp) in zip(group, scored):
        stat = gs_ref[half:, cs].astype(F32)
        m0 = stat[0:1]
        l0 = stat[1:2] + stat[2:3] + stat[3:4]
        d0 = stat[4:5] + stat[5:6] + stat[6:7]
        s = s + bias
        m = jnp.maximum(m0, jnp.max(s, axis=0, keepdims=True))
        e = jnp.exp(s - m)
        a = jnp.exp(m0 - m)
        l = a * l0 + jnp.sum(e, axis=0, keepdims=True)
        d = a * d0 + jnp.sum(e * dp, axis=0, keepdims=True)
        inv = 1.0 / jnp.where(l > 0, l, 1.0)
        prob = e * inv
        graded.append((qq, gg, prob.astype(BF16), (prob * (dp - d * inv)).astype(BF16)))
    for cs, (qq, gg, prob, ds) in zip(group, graded):
        add(cs, nn(ds, qq), nn(prob, gg))


def groups(cols, size):
    pairs = [slice(p * PAIR, (p + 1) * PAIR) for p in range(cols // PAIR)]
    return [pairs[i : i + size] for i in range(0, len(pairs), size)]


def flush(triples):
    copies = [pltpu.make_async_copy(*t) for t in triples]
    for copy in copies:
        copy.start()
    return copies


def within_kernel(bias_ref, q_ref, k_ref, v_ref, g_ref, kn_ref, vn_ref, qn_ref, gs_ref, dq_out, dk_ref, dv_ref, dq_ref, sems):
    rows, cols = k_ref.shape
    rs = side_rows(False, rows // 2)

    def put(cs, dk, dv):
        dk_ref[:, cs] = dk
        dv_ref[:, cs] = dv

    def add(cs, dk, dv):
        dk_ref[rs, cs] = dk_ref[rs, cs] + dk
        dv_ref[rs, cs] = dv_ref[rs, cs] + dv

    for group in groups(cols, OWN_GROUP):
        own_half(rs, group, bias_ref, q_ref, k_ref, v_ref, g_ref, kn_ref, vn_ref, dq_ref, put)
    copies = flush([(dq_ref, dq_out.at[rs], sems.at[0])])
    for group in groups(cols, 8):
        edge(rs, group, bias_ref, k_ref, v_ref, qn_ref, gs_ref, add)
    for copy in copies:
        copy.wait()


def across_kernel(bias_ref, q_ref, k_ref, v_ref, g_ref, kv_ref, dka_ref, dva_ref, dq_in, dq_out, dk_out, dv_out, dk_ref, dv_ref, dq_ref, dkn_ref, dvn_ref, sems):
    rows, cols = k_ref.shape
    half = rows // 2
    rs, rest = side_rows(True, half), side_rows(False, half)
    odd = lax.rem(flat_index(), 2)

    def put(cs, dk, dv):
        for part, acc, mine, other in ((dk, dka_ref, dk_ref, dkn_ref), (dv, dva_ref, dv_ref, dvn_ref)):
            part = part + acc[:, cs]
            low, high = part[:half], part[half:]
            mine[:, cs] = jnp.where(odd == 1, high, low)
            other[:, cs] = jnp.where(odd == 1, low, high).astype(BF16)

    for group in groups(cols, OWN_GROUP):
        own_half(rs, group, bias_ref, q_ref, k_ref, v_ref, g_ref, kv_ref.at[:half], kv_ref.at[half:], dq_ref, put)
    copies = flush([(dq_ref, dq_out.at[rs], sems.at[0]), (dkn_ref, dk_out.at[rest], sems.at[1]), (dvn_ref, dv_out.at[rest], sems.at[2])])
    for copy in copies:
        copy.wait()


def last_kernel(bias_ref, k_ref, v_ref, qs_ref, dka_ref, dva_ref, dk_in, dv_in, dk_out, dv_out, dk_ref, dv_ref, sems):
    rows, cols = k_ref.shape
    rs = side_rows(True, rows // 2)

    def put(cs, dk, dv):
        dv_ref[:, cs] = (dva_ref[:, cs] + dv).astype(BF16)
        dk_ref[:, cs] = (dka_ref[:, cs] + dk).astype(BF16)

    for group in groups(cols, 8):
        edge(rs, group, bias_ref, k_ref, v_ref, qs_ref.at[: rows // 2], qs_ref.at[rows // 2 :], put)
    copies = flush([(dk_ref, dk_out.at[rs], sems.at[0]), (dv_ref, dv_out.at[rs], sems.at[1])])
    for copy in copies:
        copy.wait()


VM = pl.BlockSpec(memory_space=pltpu.VMEM)
HB = pl.BlockSpec(memory_space=pl.ANY)


def body(queries, key_vectors, value_vectors, grad_output, lengths):
    rows, cols = queries.shape
    half = rows // 2
    count = lax.axis_size("blk") * lax.axis_size("head")
    across = [(a, b) for i in range(1, count - 1, 2) for a, b in ((i, i + 1), (i + 1, i))]
    within = [(a, b) for i in range(0, count, 2) for a, b in ((i, i + 1), (i + 1, i))]

    sds = jax.ShapeDtypeStruct
    whole, part, sent = sds((rows, cols), BF16), sds((half, cols), F32), sds((rows + STATS, cols), BF16)
    low_s, sent_e = sds((half, cols), BF16), sds((half + STATS, cols), BF16)
    masks = sds((2 * rows, rows), F32)
    low = pltpu.VMEM((half, cols), BF16)
    dma = pltpu.SemaphoreType.DMA((3,))

    def call(kernel, out_shape, in_specs, out_specs, scratch, flops, alias={}):
        return pl.pallas_call(
            kernel,
            out_shape=out_shape,
            in_specs=in_specs,
            out_specs=out_specs,
            scratch_shapes=scratch,
            input_output_aliases=alias,
            compiler_params=pltpu.CompilerParams(vmem_limit_bytes=20 << 20),
            cost_estimate=pl.CostEstimate(flops=flops, bytes_accessed=max(flops >> 10, 1), transcendentals=0),
        )

    k, v, kv_o, k_e, v_e, own_bias, bias_o, bias_e = call(
        prep_kernel,
        (whole,) * 3 + (low_s, low_s, sds((rows, rows), F32), masks, masks),
        [HB] * 3,
        (VM,) * 8,
        [pltpu.SMEM(lengths.shape, jnp.int32), dma],
        1 << 20,
    )(*(pltpu.with_memory_space_constraint(x, pltpu.HBM) for x in (lengths, key_vectors, value_vectors)))
    kv_o = lax.ppermute(kv_o, AXES, across)
    k_e = lax.ppermute(k_e, AXES, within)
    v_e = lax.ppermute(v_e, AXES, within)
    q, g = queries, grad_output
    qs_o, q_e, gs_e = call(local_kernel, (sent, low_s, sent_e), [VM] * 5, (VM,) * 3, [], 1 << 28)(own_bias, q, k, v, g)
    qs_o = lax.ppermute(qs_o, AXES, across)
    q_e = lax.ppermute(q_e, AXES, within)
    gs_e = lax.ppermute(gs_e, AXES, within)
    acc = sds((rows, cols), F32)
    dq, dk, dv = call(within_kernel, (whole, acc, acc), [VM] * 9, (HB, VM, VM), [low, dma], 0)(
        bias_e, q, k, v, g, k_e, v_e, q_e, gs_e
    )
    dq, dk_out, dv_out, dk, dv = call(
        across_kernel, (whole,) * 3 + (part,) * 2, [VM] * 8 + [HB], (HB,) * 3 + (VM,) * 2, [low] * 3 + [dma], 1 << 31, {8: 0}
    )(bias_o, q, k, v, g, kv_o, dk, dv, dq)
    dk, dv = call(last_kernel, (whole,) * 2, [VM] * 6 + [HB] * 2, (HB,) * 2, [low] * 2 + [dma], 1 << 27, {6: 0, 7: 1})(
        bias_o, k, v, qs_o, dk, dv, dk_out, dv_out
    )
    return dq, dk, dv


def solution(mesh):
    return jax.shard_map(
        body,
        mesh=mesh,
        in_specs=(P(AXES, None),) * 4 + (P(),),
        out_specs=(P(AXES, None),) * 3,
        check_vma=False,
    )
```

time: 21.1 us -> 20 us (0.948)
  local copies, waits for them, and re-layouts: 1.42 us -> 0.01 us
  starting transfers between devices: 8.94 us -> 7.81 us
  waiting for transfers between devices: 2.63 us -> 3.57 us
  Pallas kernels: 7.17 us -> 7.7 us
    ppermute x3 -> x5, starting transfers between devices: 6.39 us -> 5.03 us  [the longest x1 3.71 us: body(): kv_o = lax.ppermute(kv_o, AXES, across)]
    dynamic_slice x1 -> x0, local copies, waits for them, and re-layouts: 1.14 us -> none  [edges(): lax.dynamic_slice_in_dim(x, side * half, half, 0)]
    ppermute x1, waiting for transfers between devices: 2.59 us -> 3.55 us  [body(): qs_o = lax.ppermute(qs_o, AXES, across)]
    pallas_call x3 -> x5, Pallas kernels: 7.17 us -> 7.7 us  [the longest x1 2.31 us: body(): call(within_kernel, (whole, acc, acc), [VM] * 9, (HB, VM, VM), [low, dma]...]
    unnamed x10 -> x4, local copies, waits for them, and re-layouts: 0.29 us -> 0.01 us
    ppermute x1, starting transfers between devices: 2.56 us -> 2.79 us  [body(): qs_o = lax.ppermute(qs_o, AXES, across)]
  transfers between devices with their start and end apart: 4 -> 6, of which waited for: 1 -> 1; matrix products, arithmetic and copies ran while one was open for 0% -> 0% of each run, Pallas kernels for 25% -> 26%
where the time goes in v3:
time: 20 us; the launch traced here: 19.8 us
  starting transfers between devices  7.81 us (39%)
  Pallas kernels  7.7 us (38%)
  waiting for transfers between devices  3.57 us (18%)
  between operations  0.72 us (4%)
    ppermute x1, starting transfers between devices, body(): kv_o = lax.ppermute(kv_o, AXES, across)  3.71 us
    ppermute x1, waiting for transfers between devices, body(): qs_o = lax.ppermute(qs_o, AXES, across)  3.55 us
    ppermute x1, starting transfers between devices, body(): qs_o = lax.ppermute(qs_o, AXES, across)  2.79 us
    pallas_call x1, Pallas kernels, body(): call(within_kernel, (whole, acc, acc), [VM] * 9, (HB, VM, VM), [low, dma]...  2.31 us
    pallas_call x1, Pallas kernels, body(): call(across_kernel, (whole,) * 3 + (part,) * 2, [VM] * 8 + [HB], (HB,) *...  2.12 us
    pallas_call x1, Pallas kernels, body(): call(last_kernel, (whole,) * 2, [VM] * 6 + [HB] * 2, (HB,) * 2, [low] * 2...  1.4 us
    pallas_call x1, Pallas kernels, body(): call(prep_kernel, (whole,) * 3 + (low_s, low_s, sds((rows, rows), F32), m...  1.13 us
    pallas_call x1, Pallas kernels, body(): call(local_kernel, (sent, low_s, sent_e), [VM] * 5, (VM,) * 3, [], 1 << 28)  0.74 us
  transfers between devices with their start and end apart: 6, of which 1 were waited for; matrix products, arithmetic and copies ran while one was open for 0% of the time, Pallas kernels for 26%

profile of v3, /device:TPU:25, one launch (start us, length us, event | category | flops | bytes accessed | tf_op | source)
XLA Modules:
  0.0 19.8 jit_solution(6763873451131108487)
XLA Ops:
  0.6 0.0 copy-start.1
  0.6 0.0 copy-start
  0.7 1.1 %shard_map.76 = (bf16[128,1024]{1,0:T(8,128)(2,1)S(1)}, bf16[128,1024]{1,0:T(8,128)(2,1)S(1)}, bf16[128,1024]{1,0:T(8,128)(2,1)S(1)}, bf16[64,1024]{1,0:T(8,128)...) custom-call(s32[4]{0:T(128)} %len_hbm.1, ...), custom_call_target="tpu_custom_call" | custom-call | flops 1048576 | bytes 1024 | tf_op jit(solution)/shard_map/pallas_call | solution.py:281
  1.8 3.7 %collective-permute-start = (bf16[128,1024]{1,0:T(8,128)(2,1)S(1)}, bf16[128,1024]{1,0:T(8,128)(2,1)S(1)}, u32[]{:S(2)}, u32[]{:S(2)}) collective-permute-start(bf16[128,1024]{1,0:T(8,128)(2,1)S(1)} %get-tuple-element.27), channel_id=1, source_target_pairs={{1,2},{2,1},{3,4},{4,3},{5,6},{6,5},{7,8},{8,7},{9,10},{10,9},{11,... | collective-permute-start | bytes 786440 | tf_op jit(solution)/shard_map/ppermute | solution.py:289
  5.5 0.7 %collective-permute-start.1 = (bf16[64,1024]{1,0:T(8,128)(2,1)S(1)}, bf16[64,1024]{1,0:T(8,128)(2,1)S(1)}, u32[]{:S(2)}, u32[]{:S(2)}) collective-permute-start(bf16[64,1024]{1,0:T(8,128)(2,1)S(1)} %get-tuple-element.29), channel_id=1, source_target_pairs={{0,1},{1,0},{2,3},{3,2},{4,5},{5,4},{6,7},{7,6},{8,9},{9,8},{10,11... | collective-permute-start | bytes 393224 | tf_op jit(solution)/shard_map/ppermute | solution.py:290
  6.2 0.0 copy-done.1
  6.2 0.0 copy-done
  6.2 0.7 %shard_map.77 = (bf16[136,1024]{1,0:T(8,128)(2,1)S(1)}, bf16[64,1024]{1,0:T(8,128)(2,1)S(1)}, bf16[72,1024]{1,0:T(8,128)(2,1)S(1)}) custom-call(f32[128,128]{1,0:T(8,128)S(1)} %get-tuple-element.31.bias_ref, bf16[128,1024]{1,0:T(8,128)(2,1)S(1)} %copy-done, bf16[128,1024]{1,0:T(8,128)(2,1)S(1)} %get-tuple-element.25.k_ref, ...), custom_call_target="tpu_custom_call" | custom-call | flops 268435456 | bytes 262144 | tf_op jit(solution)/shard_map/pallas_call | solution.py:293
  7.0 0.0 collective-permute-start.4
  7.0 0.5 %collective-permute-start.2 = (bf16[64,1024]{1,0:T(8,128)(2,1)S(1)}, bf16[64,1024]{1,0:T(8,128)(2,1)S(1)}, u32[]{:S(2)}, u32[]{:S(2)}) collective-permute-start(bf16[64,1024]{1,0:T(8,128)(2,1)S(1)} %get-tuple-element.30), channel_id=1, source_target_pairs={{0,1},{1,0},{2,3},{3,2},{4,5},{5,4},{6,7},{7,6},{8,9},{9,8},{10,11... | collective-permute-start | bytes 393224 | tf_op jit(solution)/shard_map/ppermute | solution.py:291
  7.5 0.1 collective-permute-start.3
  7.6 0.0 collective-permute-done.1.kn_ref
  7.6 2.8 %collective-permute-start.5 = (bf16[136,1024]{1,0:T(8,128)(2,1)S(1)}, bf16[136,1024]{1,0:T(8,128)(2,1)S(1)}, u32[]{:S(2)}, u32[]{:S(2)}) collective-permute-start(bf16[136,1024]{1,0:T(8,128)(2,1)S(1)} %get-tuple-element.38), channel_id=1, source_target_pairs={{1,2},{2,1},{3,4},{4,3},{5,6},{6,5},{7,8},{8,7},{9,10},{10,9},{11,... | collective-permute-start | bytes 835592 | tf_op jit(solution)/shard_map/ppermute | solution.py:294
  10.4 0.0 collective-permute-done.2.vn_ref
  10.4 0.0 collective-permute-done.3.qn_ref
  10.4 0.0 collective-permute-done.4.gs_ref
  10.4 2.3 %shard_map.78 = (bf16[128,1024]{1,0:T(8,128)(2,1)}, f32[128,1024]{1,0:T(8,128)S(1)}, f32[128,1024]{1,0:T(8,128)S(1)}) custom-call(f32[256,128]{1,0:T(8,128)S(1)} %get-tuple-element.28.bias_ref, bf16[128,1024]{1,0:T(8,128)(2,1)S(1)} %copy-done, bf16[128,1024]{1,0:T(8,128)(2,1)S(1)} %get-tuple-element.25.k_ref, bf16[128,1024]{1,0:T(8,128)(2,1)S(1)} %get-tuple-element.26.v_ref, ...), custom_call_target="tpu_custom_call" | custom-call | bytes 1 | tf_op jit(solution)/shard_map/pallas_call | solution.py:298
  12.7 0.0 collective-permute-done.kv_ref
  12.7 2.1 %shard_map.79 = (bf16[128,1024]{1,0:T(8,128)(2,1)}, bf16[128,1024]{1,0:T(8,128)(2,1)}, bf16[128,1024]{1,0:T(8,128)(2,1)}, f32[64,1024]{1,0:T(8,128)S(1)}, f32[64,1024]{1,0:T(8,128)S(1)}) custom-call(f32[256,128]{1,0:T(8,128)S(1)} %get-tuple-element.24.bias_ref, bf16[128,1024]{1,0:T(8,128)(2,1)S(1)} %copy-done, ...), custom_call_target="tpu_custom_call", output_to_operand_aliasing={{0}: (8, {})} | custom-call | flops 2147483648 | bytes 2097152 | tf_op jit(solution)/shard_map/pallas_call | solution.py:301
  14.9 3.6 %collective-permute-done.5.qs_ref = bf16[136,1024]{1,0:T(8,128)(2,1)S(1)} collective-permute-done((bf16[136,1024]{1,0:T(8,128)(2,1)S(1)}, bf16[136,1024]{1,0:T(8,128)(2,1)S(1)}, u32[]{:S(2)}, u32[]{:S(2)}) %collective-permute-start.5) | collective-permute-done | bytes 278560 | tf_op jit(solution)/shard_map/ppermute | solution.py:294
  18.4 1.4 %shard_map.80 = (bf16[128,1024]{1,0:T(8,128)(2,1)}, bf16[128,1024]{1,0:T(8,128)(2,1)}) custom-call(f32[256,128]{1,0:T(8,128)S(1)} %get-tuple-element.24.bias_ref, bf16[128,1024]{1,0:T(8,128)(2,1)S(1)} %get-tuple-element.25.k_ref, bf16[128,1024]{1,0:T(8,128)(2,1)S(1)} %get-tuple-element.26.v_ref, ...), custom_call_target="tpu_custom_call", output_to_operand_aliasing={{0}: (6, {}), {1}: (7, {})} | custom-call | flops 134217728 | bytes 131072 | tf_op jit(solution)/shard_map/pallas_call | solution.py:304
Async XLA Ops:
  0.6 5.6 %copy-start.1 = (bf16[128,1024]{1,0:T(8,128)(2,1)S(1)}, bf16[128,1024]{1,0:T(8,128)(2,1)}, u32[]{:S(2)}) copy-start(bf16[128,1024]{1,0:T(8,128)(2,1)} %g_ref.5) | copy-start | bytes 786436
  0.6 5.6 %copy-start = (bf16[128,1024]{1,0:T(8,128)(2,1)S(1)}, bf16[128,1024]{1,0:T(8,128)(2,1)}, u32[]{:S(2)}) copy-start(bf16[128,1024]{1,0:T(8,128)(2,1)} %q_ref.5) | copy-start | bytes 786436
  1.8 10.9 %collective-permute-start = (bf16[128,1024]{1,0:T(8,128)(2,1)S(1)}, bf16[128,1024]{1,0:T(8,128)(2,1)S(1)}, u32[]{:S(2)}, u32[]{:S(2)}) collective-permute-start(bf16[128,1024]{1,0:T(8,128)(2,1)S(1)} %get-tuple-element.27), channel_id=1, source_target_pairs={{1,2},{2,1},{3,4},{4,3},{5,6},{6,5},{7,8},{8,7},{9,10},{10,9},{11,... | collective-permute-start | bytes 786440 | tf_op jit(solution)/shard_map/ppermute | solution.py:289
  5.5 2.1 %collective-permute-start.1 = (bf16[64,1024]{1,0:T(8,128)(2,1)S(1)}, bf16[64,1024]{1,0:T(8,128)(2,1)S(1)}, u32[]{:S(2)}, u32[]{:S(2)}) collective-permute-start(bf16[64,1024]{1,0:T(8,128)(2,1)S(1)} %get-tuple-element.29), channel_id=1, source_target_pairs={{0,1},{1,0},{2,3},{3,2},{4,5},{5,4},{6,7},{7,6},{8,9},{9,8},{10,11... | collective-permute-start | bytes 393224 | tf_op jit(solution)/shard_map/ppermute | solution.py:290
  7.0 3.4 %collective-permute-start.4 = (bf16[72,1024]{1,0:T(8,128)(2,1)S(1)}, bf16[72,1024]{1,0:T(8,128)(2,1)S(1)}, u32[]{:S(2)}, u32[]{:S(2)}) collective-permute-start(bf16[72,1024]{1,0:T(8,128)(2,1)S(1)} %get-tuple-element.33), channel_id=1, source_target_pairs={{0,1},{1,0},{2,3},{3,2},{4,5},{5,4},{6,7},{7,6},{8,9},{9,8},{10,11... | collective-permute-start | bytes 442376 | tf_op jit(solution)/shard_map/ppermute | solution.py:296
  7.0 3.4 %collective-permute-start.2 = (bf16[64,1024]{1,0:T(8,128)(2,1)S(1)}, bf16[64,1024]{1,0:T(8,128)(2,1)S(1)}, u32[]{:S(2)}, u32[]{:S(2)}) collective-permute-start(bf16[64,1024]{1,0:T(8,128)(2,1)S(1)} %get-tuple-element.30), channel_id=1, source_target_pairs={{0,1},{1,0},{2,3},{3,2},{4,5},{5,4},{6,7},{7,6},{8,9},{9,8},{10,11... | collective-permute-start | bytes 393224 | tf_op jit(solution)/shard_map/ppermute | solution.py:291
  7.5 2.9 %collective-permute-start.3 = (bf16[64,1024]{1,0:T(8,128)(2,1)S(1)}, bf16[64,1024]{1,0:T(8,128)(2,1)S(1)}, u32[]{:S(2)}, u32[]{:S(2)}) collective-permute-start(bf16[64,1024]{1,0:T(8,128)(2,1)S(1)} %get-tuple-element.32), channel_id=1, source_target_pairs={{0,1},{1,0},{2,3},{3,2},{4,5},{5,4},{6,7},{7,6},{8,9},{9,8},{10,11... | collective-permute-start | bytes 393224 | tf_op jit(solution)/shard_map/ppermute | solution.py:295
  7.6 10.8 %collective-permute-start.5 = (bf16[136,1024]{1,0:T(8,128)(2,1)S(1)}, bf16[136,1024]{1,0:T(8,128)(2,1)S(1)}, u32[]{:S(2)}, u32[]{:S(2)}) collective-permute-start(bf16[136,1024]{1,0:T(8,128)(2,1)S(1)} %get-tuple-element.38), channel_id=1, source_target_pairs={{1,2},{2,1},{3,4},{4,3},{5,6},{6,5},{7,8},{8,7},{9,10},{10,9},{11,... | collective-permute-start | bytes 835592 | tf_op jit(solution)/shard_map/ppermute | solution.py:294

commit v4 on v3

--- a/solution.py
+++ b/solution.py
@@ -11,7 +11,9 @@
 WIN = 64
 PAIR = 2 * DH
 STATS = 8
-OWN_GROUP = 8
+MOVED = 16
+COSTS = (1 << 28, 0, 1 << 31, 0, 1 << 27)
+LAST = 2
 SCALE = DH ** (-0.5)
 NEG = -1e30
 AXES = ("blk", "head")
@@ -64,7 +66,7 @@
     return [hi, mid, x - hi - mid]
 
 
-def prep_kernel(len_hbm, k_hbm, v_hbm, k_ref, v_ref, kv_o, k_e, v_e, own_bias, bias_o, bias_e, len_ref, sems):
+def prep_kernel(len_hbm, k_hbm, v_hbm, k_ref, v_ref, kv_o, kv_e, own_bias, bias_o, bias_e, len_ref, sems):
     copies = [
         pltpu.make_async_copy(len_hbm, len_ref, sems.at[0]),
         pltpu.make_async_copy(k_hbm, k_ref, sems.at[1]),
@@ -84,20 +86,24 @@
         out[:rows, :] = bias_of(base, mine, rows, rows, half, len_ref)
         out[rows : rows + half, :] = bias_of(other, mine, half, rows, half, len_ref)
         out[rows + half :, :] = bias_of(mine, other, half, rows, half, len_ref)
-    for n, (ref, out) in enumerate(((k_ref, k_e), (v_ref, v_e))):
+    for n, ref in enumerate((k_ref, v_ref)):
         copies[n + 1].wait()
         kv_o[n * half : (n + 1) * half, :] = ref[pl.ds(pl.multiple_of(odd * half, half), half), :]
-        out[...] = ref[pl.ds(pl.multiple_of((1 - odd) * half, half), half), :]
-
-
-def local_kernel(bias_ref, q_ref, k_ref, v_ref, g_ref, qs_o, q_e, gs_e):
+        size = half - n * MOVED
+        kv_e[n * half : n * half + size, :] = ref[pl.ds(pl.multiple_of((1 - odd) * half, half), size), :]
+
+
+def local_kernel(bias_ref, q_ref, k_ref, v_ref, g_ref, qs_1, qs_2, q_e, gs_e):
     rows, cols = q_ref.shape
     odd = lax.rem(flat_index(), 2)
     half = rows // 2
     first, other = pl.multiple_of(odd * half, half), pl.multiple_of((1 - odd) * half, half)
-    qs_o[:half, :] = q_ref[pl.ds(first, half), :] * BF16(SCALE)
-    qs_o[half:rows, :] = g_ref[pl.ds(first, half), :]
-    q_e[...] = q_ref[pl.ds(other, half), :] * BF16(SCALE)
+    cut = qs_1.shape[1]
+    for out, cs in ((qs_1, slice(0, cut)), (qs_2, slice(cut, cols))):
+        out[:half, :] = q_ref[pl.ds(first, half), cs] * BF16(SCALE)
+        out[half:rows, :] = g_ref[pl.ds(first, half), cs]
+    q_e[:half, :] = q_ref[pl.ds(other, half), :] * BF16(SCALE)
+    q_e[half:, :] = v_ref[pl.ds(pl.multiple_of(other + half - MOVED, MOVED), MOVED), :]
     gs_e[:half, :] = g_ref[pl.ds(other, half), :]
     bias = bias_ref[...]
     bias = jnp.concatenate([bias, bias], axis=1)
@@ -116,7 +122,8 @@
         a, b = stat[:, :rows], stat[:, rows:]
         lo = jnp.where(lane < half, a, pltpu.roll(b, half, 1))
         hi = jnp.where(lane < half, pltpu.roll(a, half, 1), b)
-        qs_o[rows:, cs] = jnp.where(odd == 1, hi, lo).astype(BF16)
+        out, start = (qs_1, p * PAIR) if p * PAIR < cut else (qs_2, p * PAIR - cut)
+        out[rows:, start : start + PAIR] = jnp.where(odd == 1, hi, lo).astype(BF16)
         gs_e[half:, cs] = jnp.where(odd == 1, lo, hi).astype(BF16)
 
 
@@ -125,7 +132,7 @@
     return pl.ds(pl.multiple_of((odd if across else 1 - odd) * half, half), half)
 
 
-def own_half(rs, group, bias_ref, q_ref, k_ref, v_ref, g_ref, kn_ref, vn_ref, dq_ref, add):
+def own_half(rs, group, bias_ref, q_ref, k_ref, v_ref, g_ref, kn_ref, v_near, dq_ref, add):
     rows = k_ref.shape[0]
     half = rows // 2
     lane = lax.broadcasted_iota(jnp.int32, (half, PAIR), 1)
@@ -135,7 +142,7 @@
         qq = split_heads(q_ref[rs, cs]) * BF16(SCALE)
         gg = split_heads(g_ref[rs, cs])
         s = nt(k_ref[:, cs], qq), nt(kn_ref[:, cs], qq)
-        dp = nt(v_ref[:, cs], gg), nt(vn_ref[:, cs], gg)
+        dp = nt(v_ref[:, cs], gg), nt(v_near(cs), gg)
         scored.append((qq, gg, s, dp))
     graded = []
     for qq, gg, s, dp in scored:
@@ -153,17 +160,18 @@
         dq_ref[:, cs] = (jnp.where(lane < DH, dq2[:half], dq2[half:]) * SCALE).astype(BF16)
 
 
-def edge(rs, group, bias_ref, k_ref, v_ref, qn_ref, gs_ref, add):
+def edge(rs, group, first, bias_ref, k_ref, v_ref, qn_ref, gs_ref, add):
     rows = k_ref.shape[0]
     half = rows // 2
     bias = bias_ref[rows + half :, :]
     scored = []
     for cs in group:
-        qq, gg = split_heads(qn_ref[:, cs]), split_heads(gs_ref[:half, cs])
+        ns = slice(cs.start - first, cs.stop - first)
+        qq, gg = split_heads(qn_ref[:, ns]), split_heads(gs_ref[:half, ns])
         scored.append((qq, gg, nt(k_ref[rs, cs], qq), nt(v_ref[rs, cs], gg)))
     graded = []
     for cs, (qq, gg, s, dp) in zip(group, scored):
-        stat = gs_ref[half:, cs].astype(F32)
+        stat = gs_ref[half:, cs.start - first : cs.stop - first].astype(F32)
         m0 = stat[0:1]
         l0 = stat[1:2] + stat[2:3] + stat[3:4]
         d0 = stat[4:5] + stat[5:6] + stat[6:7]
@@ -180,21 +188,14 @@
         add(cs, nn(ds, qq), nn(prob, gg))
 
 
-def groups(cols, size):
-    pairs = [slice(p * PAIR, (p + 1) * PAIR) for p in range(cols // PAIR)]
-    return [pairs[i : i + size] for i in range(0, len(pairs), size)]
-
-
-def flush(triples):
-    copies = [pltpu.make_async_copy(*t) for t in triples]
-    for copy in copies:
-        copy.start()
-    return copies
-
-
-def within_kernel(bias_ref, q_ref, k_ref, v_ref, g_ref, kn_ref, vn_ref, qn_ref, gs_ref, dq_out, dk_ref, dv_ref, dq_ref, sems):
+def pairs_of(first, end):
+    return [slice(c, c + PAIR) for c in range(first, end, PAIR)]
+
+
+def within_kernel(bias_ref, q_ref, k_ref, v_ref, g_ref, kv_ref, qn_ref, gs_ref, dq_ref, dk_ref, dv_ref):
     rows, cols = k_ref.shape
-    rs = side_rows(False, rows // 2)
+    half = rows // 2
+    rs = side_rows(False, half)
 
     def put(cs, dk, dv):
         dk_ref[:, cs] = dk
@@ -204,19 +205,18 @@
         dk_ref[rs, cs] = dk_ref[rs, cs] + dk
         dv_ref[rs, cs] = dv_ref[rs, cs] + dv
 
-    for group in groups(cols, OWN_GROUP):
-        own_half(rs, group, bias_ref, q_ref, k_ref, v_ref, g_ref, kn_ref, vn_ref, dq_ref, put)
-    copies = flush([(dq_ref, dq_out.at[rs], sems.at[0])])
-    for group in groups(cols, 8):
-        edge(rs, group, bias_ref, k_ref, v_ref, qn_ref, gs_ref, add)
-    for copy in copies:
-        copy.wait()
-
-
-def across_kernel(bias_ref, q_ref, k_ref, v_ref, g_ref, kv_ref, dka_ref, dva_ref, dq_in, dq_out, dk_out, dv_out, dk_ref, dv_ref, dq_ref, dkn_ref, dvn_ref, sems):
+    kn_ref = kv_ref.at[:half]
+
+    def vn_ref(cs):
+        return jnp.concatenate([kv_ref[half:, cs], qn_ref[half:, cs]], axis=0)
+
+    own_half(rs, pairs_of(0, cols), bias_ref, q_ref, k_ref, v_ref, g_ref, kn_ref, vn_ref, dq_ref, put)
+    edge(rs, pairs_of(0, cols), 0, bias_ref, k_ref, v_ref, qn_ref.at[:half], gs_ref, add)
+
+
+def across_kernel(bias_ref, q_ref, k_ref, v_ref, g_ref, kv_ref, dka_ref, dva_ref, dq_ref, dkn_ref, dvn_ref, dk_ref, dv_ref):
     rows, cols = k_ref.shape
     half = rows // 2
-    rs, rest = side_rows(True, half), side_rows(False, half)
     odd = lax.rem(flat_index(), 2)
 
     def put(cs, dk, dv):
@@ -226,24 +226,69 @@
             mine[:, cs] = jnp.where(odd == 1, high, low)
             other[:, cs] = jnp.where(odd == 1, low, high).astype(BF16)
 
-    for group in groups(cols, OWN_GROUP):
-        own_half(rs, group, bias_ref, q_ref, k_ref, v_ref, g_ref, kv_ref.at[:half], kv_ref.at[half:], dq_ref, put)
-    copies = flush([(dq_ref, dq_out.at[rs], sems.at[0]), (dkn_ref, dk_out.at[rest], sems.at[1]), (dvn_ref, dv_out.at[rest], sems.at[2])])
-    for copy in copies:
-        copy.wait()
-
-
-def last_kernel(bias_ref, k_ref, v_ref, qs_ref, dka_ref, dva_ref, dk_in, dv_in, dk_out, dv_out, dk_ref, dv_ref, sems):
+    own_half(
+        side_rows(True, half),
+        pairs_of(0, cols),
+        bias_ref,
+        q_ref,
+        k_ref,
+        v_ref,
+        g_ref,
+        kv_ref.at[:half],
+        lambda cs: kv_ref[half:, cs],
+        dq_ref,
+        put,
+    )
+
+
+def edge_into(first, bias_ref, k_ref, v_ref, qs_ref, dka_ref, dva_ref, dk_ref, dv_ref):
+    half = k_ref.shape[0] // 2
+    size = qs_ref.shape[1]
+
+    def put(cs, dk, dv):
+        to = slice(cs.start - first, cs.stop - first)
+        dv_ref[:, to] = (dva_ref[:, cs] + dv).astype(BF16)
+        dk_ref[:, to] = (dka_ref[:, cs] + dk).astype(BF16)
+
+    edge(
+        side_rows(True, half),
+        pairs_of(first, first + size),
+        first,
+        bias_ref,
+        k_ref,
+        v_ref,
+        qs_ref.at[:half],
+        qs_ref.at[half:],
+        put,
+    )
+
+
+def first_edge_kernel(bias_ref, k_ref, v_ref, qs_ref, dka_ref, dva_ref, dk_ref, dv_ref):
+    edge_into(0, bias_ref, k_ref, v_ref, qs_ref, dka_ref, dva_ref, dk_ref, dv_ref)
+
+
+def last_kernel(
+    bias_ref, k_ref, v_ref, qs_ref, dka_ref, dva_ref, dqn, dqm, dkn, dvn, dk1, dv1, dq_out, dk_out, dv_out, dk2, dv2, sems
+):
     rows, cols = k_ref.shape
-    rs = side_rows(True, rows // 2)
-
-    def put(cs, dk, dv):
-        dv_ref[:, cs] = (dva_ref[:, cs] + dv).astype(BF16)
-        dk_ref[:, cs] = (dka_ref[:, cs] + dk).astype(BF16)
-
-    for group in groups(cols, 8):
-        edge(rs, group, bias_ref, k_ref, v_ref, qs_ref.at[: rows // 2], qs_ref.at[rows // 2 :], put)
-    copies = flush([(dk_ref, dk_out.at[rs], sems.at[0]), (dv_ref, dv_out.at[rs], sems.at[1])])
+    half = rows // 2
+    mine, other = side_rows(True, half), side_rows(False, half)
+    first = cols - qs_ref.shape[1]
+    early = [
+        (dqn, dq_out.at[other]),
+        (dqm, dq_out.at[mine]),
+        (dkn, dk_out.at[other]),
+        (dvn, dv_out.at[other]),
+        (dk1, dk_out.at[mine, :first]),
+        (dv1, dv_out.at[mine, :first]),
+    ]
+    late = [(dk2, dk_out.at[mine, first:]), (dv2, dv_out.at[mine, first:])]
+    copies = [pltpu.make_async_copy(a, b, sems.at[n]) for n, (a, b) in enumerate(early + late)]
+    for copy in copies[: len(early)]:
+        copy.start()
+    edge_into(first, bias_ref, k_ref, v_ref, qs_ref, dka_ref, dva_ref, dk2, dv2)
+    for copy in copies[len(early) :]:
+        copy.start()
     for copy in copies:
         copy.wait()
 
@@ -260,51 +305,60 @@
     within = [(a, b) for i in range(0, count, 2) for a, b in ((i, i + 1), (i + 1, i))]
 
     sds = jax.ShapeDtypeStruct
-    whole, part, sent = sds((rows, cols), BF16), sds((half, cols), F32), sds((rows + STATS, cols), BF16)
-    low_s, sent_e = sds((half, cols), BF16), sds((half + STATS, cols), BF16)
+    whole, part = sds((rows, cols), BF16), sds((half, cols), F32)
+    low_s = sds((half, cols), BF16)
+    sent_q, sent_g = sds((half + MOVED, cols), BF16), sds((half + STATS, cols), BF16)
     masks = sds((2 * rows, rows), F32)
-    low = pltpu.VMEM((half, cols), BF16)
     dma = pltpu.SemaphoreType.DMA((3,))
 
-    def call(kernel, out_shape, in_specs, out_specs, scratch, flops, alias={}):
+    def call(kernel, out_shape, in_specs, out_specs, scratch, flops):
         return pl.pallas_call(
             kernel,
             out_shape=out_shape,
             in_specs=in_specs,
             out_specs=out_specs,
             scratch_shapes=scratch,
-            input_output_aliases=alias,
             compiler_params=pltpu.CompilerParams(vmem_limit_bytes=20 << 20),
             cost_estimate=pl.CostEstimate(flops=flops, bytes_accessed=max(flops >> 10, 1), transcendentals=0),
         )
 
-    k, v, kv_o, k_e, v_e, own_bias, bias_o, bias_e = call(
+    k, v, kv_o, kv_e, own_bias, bias_o, bias_e = call(
         prep_kernel,
-        (whole,) * 3 + (low_s, low_s, sds((rows, rows), F32), masks, masks),
+        (whole,) * 3 + (sds((rows - MOVED, cols), BF16), sds((rows, rows), F32), masks, masks),
         [HB] * 3,
-        (VM,) * 8,
+        (VM,) * 7,
         [pltpu.SMEM(lengths.shape, jnp.int32), dma],
         1 << 20,
     )(*(pltpu.with_memory_space_constraint(x, pltpu.HBM) for x in (lengths, key_vectors, value_vectors)))
     kv_o = lax.ppermute(kv_o, AXES, across)
-    k_e = lax.ppermute(k_e, AXES, within)
-    v_e = lax.ppermute(v_e, AXES, within)
+    kv_e = lax.ppermute(kv_e, AXES, within)
     q, g = queries, grad_output
-    qs_o, q_e, gs_e = call(local_kernel, (sent, low_s, sent_e), [VM] * 5, (VM,) * 3, [], 1 << 28)(own_bias, q, k, v, g)
-    qs_o = lax.ppermute(qs_o, AXES, across)
+    cut = cols - LAST * PAIR
+    qs_1, qs_2, q_e, gs_e = call(
+        local_kernel,
+        (sds((rows + STATS, cut), BF16), sds((rows + STATS, cols - cut), BF16), sent_q, sent_g),
+        [VM] * 5,
+        (VM,) * 4,
+        [],
+        COSTS[0],
+    )(own_bias, q, k, v, g)
+    qs_1 = lax.ppermute(qs_1, AXES, across)
+    qs_2 = lax.ppermute(qs_2, AXES, across)
     q_e = lax.ppermute(q_e, AXES, within)
     gs_e = lax.ppermute(gs_e, AXES, within)
     acc = sds((rows, cols), F32)
-    dq, dk, dv = call(within_kernel, (whole, acc, acc), [VM] * 9, (HB, VM, VM), [low, dma], 0)(
-        bias_e, q, k, v, g, k_e, v_e, q_e, gs_e
-    )
-    dq, dk_out, dv_out, dk, dv = call(
-        across_kernel, (whole,) * 3 + (part,) * 2, [VM] * 8 + [HB], (HB,) * 3 + (VM,) * 2, [low] * 3 + [dma], 1 << 31, {8: 0}
-    )(bias_o, q, k, v, g, kv_o, dk, dv, dq)
-    dk, dv = call(last_kernel, (whole,) * 2, [VM] * 6 + [HB] * 2, (HB,) * 2, [low] * 2 + [dma], 1 << 27, {6: 0, 7: 1})(
-        bias_o, k, v, qs_o, dk, dv, dk_out, dv_out
-    )
-    return dq, dk, dv
+    dqn, dk, dv = call(within_kernel, (low_s, acc, acc), [VM] * 8, (VM,) * 3, [], COSTS[1])(
+        bias_e, q, k, v, g, kv_e, q_e, gs_e
+    )
+    dqm, dkn, dvn, dk, dv = call(across_kernel, (low_s,) * 3 + (part,) * 2, [VM] * 8, (VM,) * 5, [], COSTS[2])(
+        bias_o, q, k, v, g, kv_o, dk, dv
+    )
+    done = sds((half, cut), BF16)
+    dk1, dv1 = call(first_edge_kernel, (done, done), [VM] * 6, (VM,) * 2, [], COSTS[3])(bias_o, k, v, qs_1, dk, dv)
+    rest = pltpu.VMEM((half, cols - cut), BF16)
+    return call(
+        last_kernel, (whole,) * 3, [VM] * 12, (HB,) * 3, [rest, rest, pltpu.SemaphoreType.DMA((8,))], COSTS[4]
+    )(bias_o, k, v, qs_2, dk, dv, dqn, dqm, dkn, dvn, dk1, dv1)
 
 
 def solution(mesh):

time: 20 us -> 19.7 us (0.985)
  starting transfers between devices: 7.81 us -> 10.5 us
  waiting for transfers between devices: 3.57 us -> 1.51 us
  Pallas kernels: 7.7 us -> 6.67 us
    ppermute x3, starting transfers between devices: 3.99 us -> 6.26 us  [the longest x1 2.8 us: body(): qs_1 = lax.ppermute(qs_1, AXES, across)]
    ppermute x3, waiting for transfers between devices: 3.56 us -> 1.5 us  [the longest x1 0.92 us: body(): qs_2 = lax.ppermute(qs_2, AXES, across)]
    pallas_call x5 -> x6, Pallas kernels: 7.7 us -> 6.67 us  [the longest x1 1.79 us: body(): call(within_kernel, (low_s, acc, acc), [VM] * 8, (VM,) * 3, [], COSTS[1])]
    ppermute x1, starting transfers between devices: 0.04 us -> 0.48 us  [body(): gs_e = lax.ppermute(gs_e, AXES, within)]
  transfers between devices with their start and end apart: 6 -> 6, of which waited for: 1 -> 2; matrix products, arithmetic and copies ran while one was open for 0% -> 0% of each run, Pallas kernels for 26% -> 23%
where the time goes in v4:
time: 19.7 us; the launch traced here: 19.4 us
  starting transfers between devices  10.5 us (53%)
  Pallas kernels  6.67 us (34%)
  waiting for transfers between devices  1.51 us (8%)
  between operations  0.73 us (4%)
    ppermute x1, starting transfers between devices, body(): kv_o = lax.ppermute(kv_o, AXES, across)  3.71 us
    ppermute x1, starting transfers between devices, body(): qs_1 = lax.ppermute(qs_1, AXES, across)  2.8 us
    ppermute x1, starting transfers between devices, body(): qs_2 = lax.ppermute(qs_2, AXES, across)  2.75 us
    pallas_call x1, Pallas kernels, body(): call(within_kernel, (low_s, acc, acc), [VM] * 8, (VM,) * 3, [], COSTS[1])  1.79 us
    pallas_call x1, Pallas kernels, body(): call(across_kernel, (low_s,) * 3 + (part,) * 2, [VM] * 8, (VM,) * 5, [],...  1.36 us
    pallas_call x1, Pallas kernels, body(): call(prep_kernel, (whole,) * 3 + (sds((rows - MOVED, cols), BF16), sds((r...  1.13 us
    pallas_call x1, Pallas kernels, body(): call(last_kernel, (whole,) * 3, [VM] * 12, (HB,) * 3, [rest, rest, pltpu....  1.09 us
    ppermute x1, waiting for transfers between devices, body(): qs_2 = lax.ppermute(qs_2, AXES, across)  0.92 us
  transfers between devices with their start and end apart: 6, of which 2 were waited for; matrix products, arithmetic and copies ran while one was open for 0% of the time, Pallas kernels for 23%

profile of v4, /device:TPU:25, one launch (start us, length us, event | category | flops | bytes accessed | tf_op | source)
XLA Modules:
  0.0 19.4 jit_solution(7905791574991606850)
XLA Ops:
  0.6 0.0 copy-start.1
  0.6 0.0 copy-start
  0.7 1.1 %shard_map.76 = (bf16[128,1024]{1,0:T(8,128)(2,1)S(1)}, bf16[128,1024]{1,0:T(8,128)(2,1)S(1)}, bf16[128,1024]{1,0:T(8,128)(2,1)S(1)}, bf16[112,1024]{1,0:T(8,128...) custom-call(s32[4]{0:T(128)} %len_hbm.1, bf16[128,1024]{1,0:T(8,128)(2,1)} %k_hbm.1, ...), custom_call_target="tpu_custom_call" | custom-call | flops 1048576 | bytes 1024 | tf_op jit(solution)/shard_map/pallas_call | solution.py:325
  1.8 3.7 %collective-permute-start.1 = (bf16[128,1024]{1,0:T(8,128)(2,1)S(1)}, bf16[128,1024]{1,0:T(8,128)(2,1)S(1)}, u32[]{:S(2)}, u32[]{:S(2)}) collective-permute-start(bf16[128,1024]{1,0:T(8,128)(2,1)S(1)} %get-tuple-element.29), channel_id=1, source_target_pairs={{1,2},{2,1},{3,4},{4,3},{5,6},{6,5},{7,8},{8,7},{9,10},{10,9},{11,... | collective-permute-start | bytes 786440 | tf_op jit(solution)/shard_map/ppermute | solution.py:333
  5.5 0.7 %collective-permute-start.2 = (bf16[112,1024]{1,0:T(8,128)(2,1)S(1)}, bf16[112,1024]{1,0:T(8,128)(2,1)S(1)}, u32[]{:S(2)}, u32[]{:S(2)}) collective-permute-start(bf16[112,1024]{1,0:T(8,128)(2,1)S(1)} %get-tuple-element.31), channel_id=1, source_target_pairs={{0,1},{1,0},{2,3},{3,2},{4,5},{5,4},{6,7},{7,6},{8,9},{9,8},{10,11... | collective-permute-start | bytes 688136 | tf_op jit(solution)/shard_map/ppermute | solution.py:334
  6.2 0.0 copy-done.1
  6.2 0.0 copy-done
  6.2 0.7 %shard_map.77 = (bf16[136,768]{1,0:T(8,128)(2,1)S(1)}, bf16[136,256]{1,0:T(8,128)(2,1)S(1)}, bf16[80,1024]{1,0:T(8,128)(2,1)S(1)}, bf16[72,1024]{1,0:T(8,128)(2,1)S(1)}) custom-call(f32[128,128]{1,0:T(8,128)S(1)} %get-tuple-element.27.bias_ref, bf16[128,1024]{1,0:T(8,128)(2,1)S(1)} %copy-done, bf16[128,1024]{1,0:T(8,128)(2,1)S(1)} %get-tuple-element.25.k_ref, ...), custom_call_target="tpu_custom_call" | custom-call | flops 268435456 | bytes 262144 | tf_op jit(solution)/shard_map/pallas_call | solution.py:337
  7.0 0.0 collective-permute-start.3
  7.0 0.5 %collective-permute-start.4 = (bf16[72,1024]{1,0:T(8,128)(2,1)S(1)}, bf16[72,1024]{1,0:T(8,128)(2,1)S(1)}, u32[]{:S(2)}, u32[]{:S(2)}) collective-permute-start(bf16[72,1024]{1,0:T(8,128)(2,1)S(1)} %get-tuple-element.33), channel_id=1, source_target_pairs={{0,1},{1,0},{2,3},{3,2},{4,5},{5,4},{6,7},{7,6},{8,9},{9,8},{10,11... | collective-permute-start | bytes 442376 | tf_op jit(solution)/shard_map/ppermute | solution.py:348
  7.5 2.8 %collective-permute-start.5 = (bf16[136,768]{1,0:T(8,128)(2,1)S(1)}, bf16[136,768]{1,0:T(8,128)(2,1)S(1)}, u32[]{:S(2)}, u32[]{:S(2)}) collective-permute-start(bf16[136,768]{1,0:T(8,128)(2,1)S(1)} %get-tuple-element.42), channel_id=1, source_target_pairs={{1,2},{2,1},{3,4},{4,3},{5,6},{6,5},{7,8},{8,7},{9,10},{10,9},{11,... | collective-permute-start | bytes 626696 | tf_op jit(solution)/shard_map/ppermute | solution.py:345
  10.3 0.0 collective-permute-done.4.gs_ref
  10.3 2.8 %collective-permute-start = (bf16[136,256]{1,0:T(8,128)(2,1)S(1)}, bf16[136,256]{1,0:T(8,128)(2,1)S(1)}, u32[]{:S(2)}, u32[]{:S(2)}) collective-permute-start(bf16[136,256]{1,0:T(8,128)(2,1)S(1)} %get-tuple-element.28), channel_id=1, source_target_pairs={{1,2},{2,1},{3,4},{4,3},{5,6},{6,5},{7,8},{8,7},{9,10},{10,9},{11,... | collective-permute-start | bytes 208904 | tf_op jit(solution)/shard_map/ppermute | solution.py:346
  13.1 0.0 collective-permute-done.3.qn_ref
  13.1 0.0 collective-permute-done.2.kv_ref
  13.1 1.8 %shard_map.78 = (bf16[64,1024]{1,0:T(8,128)(2,1)S(1)}, f32[128,1024]{1,0:T(8,128)S(1)}, f32[128,1024]{1,0:T(8,128)S(1)}) custom-call(f32[256,128]{1,0:T(8,128)S(1)} %get-tuple-element.30.bias_ref, bf16[128,1024]{1,0:T(8,128)(2,1)S(1)} %copy-done, bf16[128,1024]{1,0:T(8,128)(2,1)S(1)} %get-tuple-element.25.k_ref, ...), custom_call_target="tpu_custom_call" | custom-call | bytes 1 | tf_op jit(solution)/shard_map/pallas_call | solution.py:350
  14.9 0.0 collective-permute-done.1.kv_ref
  14.9 1.4 %shard_map.79 = (bf16[64,1024]{1,0:T(8,128)(2,1)S(1)}, bf16[64,1024]{1,0:T(8,128)(2,1)S(1)}, bf16[64,1024]{1,0:T(8,128)(2,1)S(1)}, f32[64,1024]{1,0:T(8,128)S(1)}, f32[64,1024]{1,0:T(8,128)S(1)}) custom-call(f32[256,128]{1,0:T(8,128)S(1)} %get-tuple-element.24.bias_ref, bf16[128,1024]{1,0:T(8,128)(2,1)S(1)} %copy-done, ...), custom_call_target="tpu_custom_call" | custom-call | flops 2147483648 | bytes 2097152 | tf_op jit(solution)/shard_map/pallas_call | solution.py:353
  16.3 0.6 %collective-permute-done.5.qs_ref = bf16[136,768]{1,0:T(8,128)(2,1)S(1)} collective-permute-done((bf16[136,768]{1,0:T(8,128)(2,1)S(1)}, bf16[136,768]{1,0:T(8,128)(2,1)S(1)}, u32[]{:S(2)}, u32[]{:S(2)}) %collective-permute-start.5) | collective-permute-done | bytes 208928 | tf_op jit(solution)/shard_map/ppermute | solution.py:345
  16.8 0.6 %shard_map.80 = (bf16[64,768]{1,0:T(8,128)(2,1)S(1)}, bf16[64,768]{1,0:T(8,128)(2,1)S(1)}) custom-call(f32[256,128]{1,0:T(8,128)S(1)} %get-tuple-element.24.bias_ref, bf16[128,1024]{1,0:T(8,128)(2,1)S(1)} %get-tuple-element.25.k_ref, bf16[128,1024]{1,0:T(8,128)(2,1)S(1)} %get-tuple-element.26.v_ref, bf16[136,768]{1,0:T(8,128)(2,1)S(1)} %collective-permute-done.5.qs_ref, ...), custom_call_target="tpu_custom_call" | custom-call | bytes 1 | tf_op jit(solution)/shard_map/pallas_call | solution.py:357
  17.4 0.9 %collective-permute-done.qs_ref = bf16[136,256]{1,0:T(8,128)(2,1)S(1)} collective-permute-done((bf16[136,256]{1,0:T(8,128)(2,1)S(1)}, bf16[136,256]{1,0:T(8,128)(2,1)S(1)}, u32[]{:S(2)}, u32[]{:S(2)}) %collective-permute-start) | collective-permute-done | bytes 69664 | tf_op jit(solution)/shard_map/ppermute | solution.py:346
  18.3 1.1 %shard_map.81 = (bf16[128,1024]{1,0:T(8,128)(2,1)}, bf16[128,1024]{1,0:T(8,128)(2,1)}, bf16[128,1024]{1,0:T(8,128)(2,1)}) custom-call(f32[256,128]{1,0:T(8,128)S(1)} %get-tuple-element.24.bias_ref, bf16[128,1024]{1,0:T(8,128)(2,1)S(1)} %get-tuple-element.25.k_ref, bf16[128,1024]{1,0:T(8,128)(2,1)S(1)} %get-tuple-element.26.v_ref, ...), custom_call_target="tpu_custom_call" | custom-call | flops 134217728 | bytes 131072 | tf_op jit(solution)/shard_map/pallas_call | solution.py:359
Async XLA Ops:
  0.6 5.6 %copy-start.1 = (bf16[128,1024]{1,0:T(8,128)(2,1)S(1)}, bf16[128,1024]{1,0:T(8,128)(2,1)}, u32[]{:S(2)}) copy-start(bf16[128,1024]{1,0:T(8,128)(2,1)} %g_ref.5) | copy-start | bytes 786436
  0.6 5.6 %copy-start = (bf16[128,1024]{1,0:T(8,128)(2,1)S(1)}, bf16[128,1024]{1,0:T(8,128)(2,1)}, u32[]{:S(2)}) copy-start(bf16[128,1024]{1,0:T(8,128)(2,1)} %q_ref.5) | copy-start | bytes 786436
  1.8 13.1 %collective-permute-start.1 = (bf16[128,1024]{1,0:T(8,128)(2,1)S(1)}, bf16[128,1024]{1,0:T(8,128)(2,1)S(1)}, u32[]{:S(2)}, u32[]{:S(2)}) collective-permute-start(bf16[128,1024]{1,0:T(8,128)(2,1)S(1)} %get-tuple-element.29), channel_id=1, source_target_pairs={{1,2},{2,1},{3,4},{4,3},{5,6},{6,5},{7,8},{8,7},{9,10},{10,9},{11,... | collective-permute-start | bytes 786440 | tf_op jit(solution)/shard_map/ppermute | solution.py:333
  5.5 7.6 %collective-permute-start.2 = (bf16[112,1024]{1,0:T(8,128)(2,1)S(1)}, bf16[112,1024]{1,0:T(8,128)(2,1)S(1)}, u32[]{:S(2)}, u32[]{:S(2)}) collective-permute-start(bf16[112,1024]{1,0:T(8,128)(2,1)S(1)} %get-tuple-element.31), channel_id=1, source_target_pairs={{0,1},{1,0},{2,3},{3,2},{4,5},{5,4},{6,7},{7,6},{8,9},{9,8},{10,11... | collective-permute-start | bytes 688136 | tf_op jit(solution)/shard_map/ppermute | solution.py:334
  7.0 6.1 %collective-permute-start.3 = (bf16[80,1024]{1,0:T(8,128)(2,1)S(1)}, bf16[80,1024]{1,0:T(8,128)(2,1)S(1)}, u32[]{:S(2)}, u32[]{:S(2)}) collective-permute-start(bf16[80,1024]{1,0:T(8,128)(2,1)S(1)} %get-tuple-element.32), channel_id=1, source_target_pairs={{0,1},{1,0},{2,3},{3,2},{4,5},{5,4},{6,7},{7,6},{8,9},{9,8},{10,11... | collective-permute-start | bytes 491528 | tf_op jit(solution)/shard_map/ppermute | solution.py:347
  7.0 3.3 %collective-permute-start.4 = (bf16[72,1024]{1,0:T(8,128)(2,1)S(1)}, bf16[72,1024]{1,0:T(8,128)(2,1)S(1)}, u32[]{:S(2)}, u32[]{:S(2)}) collective-permute-start(bf16[72,1024]{1,0:T(8,128)(2,1)S(1)} %get-tuple-element.33), channel_id=1, source_target_pairs={{0,1},{1,0},{2,3},{3,2},{4,5},{5,4},{6,7},{7,6},{8,9},{9,8},{10,11... | collective-permute-start | bytes 442376 | tf_op jit(solution)/shard_map/ppermute | solution.py:348
  7.5 9.3 %collective-permute-start.5 = (bf16[136,768]{1,0:T(8,128)(2,1)S(1)}, bf16[136,768]{1,0:T(8,128)(2,1)S(1)}, u32[]{:S(2)}, u32[]{:S(2)}) collective-permute-start(bf16[136,768]{1,0:T(8,128)(2,1)S(1)} %get-tuple-element.42), channel_id=1, source_target_pairs={{1,2},{2,1},{3,4},{4,3},{5,6},{6,5},{7,8},{8,7},{9,10},{10,9},{11,... | collective-permute-start | bytes 626696 | tf_op jit(solution)/shard_map/ppermute | solution.py:345
  10.3 8.0 %collective-permute-start = (bf16[136,256]{1,0:T(8,128)(2,1)S(1)}, bf16[136,256]{1,0:T(8,128)(2,1)S(1)}, u32[]{:S(2)}, u32[]{:S(2)}) collective-permute-start(bf16[136,256]{1,0:T(8,128)(2,1)S(1)} %get-tuple-element.28), channel_id=1, source_target_pairs={{1,2},{2,1},{3,4},{4,3},{5,6},{6,5},{7,8},{8,7},{9,10},{10,9},{11,... | collective-permute-start | bytes 208904 | tf_op jit(solution)/shard_map/ppermute | solution.py:346

commit v5 on v4

--- a/solution.py
+++ b/solution.py
@@ -11,6 +11,7 @@
 WIN = 64
 PAIR = 2 * DH
 STATS = 8
+FAR_STATS = (0, 1, 2, 4, 5, 6)
 MOVED = 16
 COSTS = (1 << 28, 0, 1 << 31, 0, 1 << 27)
 LAST = 2
@@ -108,6 +109,7 @@
     bias = bias_ref[...]
     bias = jnp.concatenate([bias, bias], axis=1)
     lane = lax.broadcasted_iota(jnp.int32, (1, rows), 1)
+    far = []
     for p in range(cols // PAIR):
         cs = slice(p * PAIR, (p + 1) * PAIR)
         qq = split_heads(q_ref[:, cs]) * BF16(SCALE)
@@ -122,9 +124,11 @@
         a, b = stat[:, :rows], stat[:, rows:]
         lo = jnp.where(lane < half, a, pltpu.roll(b, half, 1))
         hi = jnp.where(lane < half, pltpu.roll(a, half, 1), b)
-        out, start = (qs_1, p * PAIR) if p * PAIR < cut else (qs_2, p * PAIR - cut)
-        out[rows:, start : start + PAIR] = jnp.where(odd == 1, hi, lo).astype(BF16)
+        far.append(jnp.where(odd == 1, hi, lo))
         gs_e[half:, cs] = jnp.where(odd == 1, lo, hi).astype(BF16)
+    for n, r in enumerate(FAR_STATS):
+        block = jnp.concatenate([stat[r : r + 1] for stat in far], axis=0)
+        qs_1[rows:, n * PAIR : (n + 1) * PAIR] = block.astype(BF16)
 
 
 def side_rows(across, half):
@@ -160,21 +164,18 @@
         dq_ref[:, cs] = (jnp.where(lane < DH, dq2[:half], dq2[half:]) * SCALE).astype(BF16)
 
 
-def edge(rs, group, first, bias_ref, k_ref, v_ref, qn_ref, gs_ref, add):
+def edge(rs, group, first, bias_ref, k_ref, v_ref, qn_ref, g_ref, stats, add):
     rows = k_ref.shape[0]
     half = rows // 2
     bias = bias_ref[rows + half :, :]
     scored = []
     for cs in group:
         ns = slice(cs.start - first, cs.stop - first)
-        qq, gg = split_heads(qn_ref[:, ns]), split_heads(gs_ref[:half, ns])
+        qq, gg = split_heads(qn_ref[:, ns]), split_heads(g_ref[:, ns])
         scored.append((qq, gg, nt(k_ref[rs, cs], qq), nt(v_ref[rs, cs], gg)))
     graded = []
     for cs, (qq, gg, s, dp) in zip(group, scored):
-        stat = gs_ref[half:, cs.start - first : cs.stop - first].astype(F32)
-        m0 = stat[0:1]
-        l0 = stat[1:2] + stat[2:3] + stat[3:4]
-        d0 = stat[4:5] + stat[5:6] + stat[6:7]
+        m0, l0, d0 = stats(cs)
         s = s + bias
         m = jnp.maximum(m0, jnp.max(s, axis=0, keepdims=True))
         e = jnp.exp(s - m)
@@ -211,7 +212,12 @@
         return jnp.concatenate([kv_ref[half:, cs], qn_ref[half:, cs]], axis=0)
 
     own_half(rs, pairs_of(0, cols), bias_ref, q_ref, k_ref, v_ref, g_ref, kn_ref, vn_ref, dq_ref, put)
-    edge(rs, pairs_of(0, cols), 0, bias_ref, k_ref, v_ref, qn_ref.at[:half], gs_ref, add)
+
+    def stats(cs):
+        stat = gs_ref[half:, cs].astype(F32)
+        return stat[0:1], stat[1:2] + stat[2:3] + stat[3:4], stat[4:5] + stat[5:6] + stat[6:7]
+
+    edge(rs, pairs_of(0, cols), 0, bias_ref, k_ref, v_ref, qn_ref.at[:half], gs_ref.at[:half], stats, add)
 
 
 def across_kernel(bias_ref, q_ref, k_ref, v_ref, g_ref, kv_ref, dka_ref, dva_ref, dq_ref, dkn_ref, dvn_ref, dk_ref, dv_ref):
@@ -241,8 +247,16 @@
     )
 
 
-def edge_into(first, bias_ref, k_ref, v_ref, qs_ref, dka_ref, dva_ref, dk_ref, dv_ref):
-    half = k_ref.shape[0] // 2
+def edge_into(first, bias_ref, k_ref, v_ref, qs_ref, st_ref, dka_ref, dva_ref, dk_ref, dv_ref):
+    rows = k_ref.shape[0]
+    half = rows // 2
+    stat = st_ref[rows:, :].astype(F32)
+
+    def stats(cs):
+        p = cs.start // PAIR
+        m, l1, l2, d1, d2, d3 = (stat[p : p + 1, n * PAIR : (n + 1) * PAIR] for n in range(len(FAR_STATS)))
+        return m, l1 + l2, d1 + d2 + d3
+
     size = qs_ref.shape[1]
 
     def put(cs, dk, dv):
@@ -258,17 +272,18 @@
         k_ref,
         v_ref,
         qs_ref.at[:half],
-        qs_ref.at[half:],
+        qs_ref.at[half:rows],
+        stats,
         put,
     )
 
 
 def first_edge_kernel(bias_ref, k_ref, v_ref, qs_ref, dka_ref, dva_ref, dk_ref, dv_ref):
-    edge_into(0, bias_ref, k_ref, v_ref, qs_ref, dka_ref, dva_ref, dk_ref, dv_ref)
+    edge_into(0, bias_ref, k_ref, v_ref, qs_ref, qs_ref, dka_ref, dva_ref, dk_ref, dv_ref)
 
 
 def last_kernel(
-    bias_ref, k_ref, v_ref, qs_ref, dka_ref, dva_ref, dqn, dqm, dkn, dvn, dk1, dv1, dq_out, dk_out, dv_out, dk2, dv2, sems
+    bias_ref, k_ref, v_ref, qs_ref, st_ref, dka_ref, dva_ref, dqn, dqm, dkn, dvn, dk1, dv1, dq_out, dk_out, dv_out, dk2, dv2, sems
 ):
     rows, cols = k_ref.shape
     half = rows // 2
@@ -286,7 +301,7 @@
     copies = [pltpu.make_async_copy(a, b, sems.at[n]) for n, (a, b) in enumerate(early + late)]
     for copy in copies[: len(early)]:
         copy.start()
-    edge_into(first, bias_ref, k_ref, v_ref, qs_ref, dka_ref, dva_ref, dk2, dv2)
+    edge_into(first, bias_ref, k_ref, v_ref, qs_ref, st_ref, dka_ref, dva_ref, dk2, dv2)
     for copy in copies[len(early) :]:
         copy.start()
     for copy in copies:
@@ -336,7 +351,7 @@
     cut = cols - LAST * PAIR
     qs_1, qs_2, q_e, gs_e = call(
         local_kernel,
-        (sds((rows + STATS, cut), BF16), sds((rows + STATS, cols - cut), BF16), sent_q, sent_g),
+        (sds((rows + STATS, cut), BF16), sds((rows, cols - cut), BF16), sent_q, sent_g),
         [VM] * 5,
         (VM,) * 4,
         [],
@@ -357,8 +372,8 @@
     dk1, dv1 = call(first_edge_kernel, (done, done), [VM] * 6, (VM,) * 2, [], COSTS[3])(bias_o, k, v, qs_1, dk, dv)
     rest = pltpu.VMEM((half, cols - cut), BF16)
     return call(
-        last_kernel, (whole,) * 3, [VM] * 12, (HB,) * 3, [rest, rest, pltpu.SemaphoreType.DMA((8,))], COSTS[4]
-    )(bias_o, k, v, qs_2, dk, dv, dqn, dqm, dkn, dvn, dk1, dv1)
+        last_kernel, (whole,) * 3, [VM] * 13, (HB,) * 3, [rest, rest, pltpu.SemaphoreType.DMA((8,))], COSTS[4]
+    )(bias_o, k, v, qs_2, qs_1, dk, dv, dqn, dqm, dkn, dvn, dk1, dv1)
 
 
 def solution(mesh):

time: 19.7 us -> 19.6 us (level)
  no operation moved by 1% of the time
where the time goes in v5:
time: 19.6 us; the launch traced here: 19.4 us
  starting transfers between devices  10.5 us (54%)
  Pallas kernels  6.74 us (34%)
  waiting for transfers between devices  1.42 us (7%)
  between operations  0.73 us (4%)
    ppermute x1, starting transfers between devices, body(): kv_o = lax.ppermute(kv_o, AXES, across)  3.71 us
    ppermute x1, starting transfers between devices, body(): qs_1 = lax.ppermute(qs_1, AXES, across)  2.81 us
    ppermute x1, starting transfers between devices, body(): qs_2 = lax.ppermute(qs_2, AXES, across)  2.74 us
    pallas_call x1, Pallas kernels, body(): call(within_kernel, (low_s, acc, acc), [VM] * 8, (VM,) * 3, [], COSTS[1])  1.79 us
    pallas_call x1, Pallas kernels, body(): call(across_kernel, (low_s,) * 3 + (part,) * 2, [VM] * 8, (VM,) * 5, [],...  1.35 us
    pallas_call x1, Pallas kernels, body(): call(last_kernel, (whole,) * 3, [VM] * 13, (HB,) * 3, [rest, rest, pltpu....  1.15 us
    pallas_call x1, Pallas kernels, body(): call(prep_kernel, (whole,) * 3 + (sds((rows - MOVED, cols), BF16), sds((r...  1.13 us
    ppermute x1, waiting for transfers between devices, body(): qs_2 = lax.ppermute(qs_2, AXES, across)  0.83 us
  transfers between devices with their start and end apart: 6, of which 2 were waited for; matrix products, arithmetic and copies ran while one was open for 0% of the time, Pallas kernels for 23%

profile of v5, /device:TPU:25, one launch (start us, length us, event | category | flops | bytes accessed | tf_op | source)
XLA Modules:
  0.0 19.4 jit_solution(5386826530918105594)
XLA Ops:
  0.6 0.0 copy-start.1
  0.6 0.0 copy-start
  0.7 1.1 %shard_map.76 = (bf16[128,1024]{1,0:T(8,128)(2,1)S(1)}, bf16[128,1024]{1,0:T(8,128)(2,1)S(1)}, bf16[128,1024]{1,0:T(8,128)(2,1)S(1)}, bf16[112,1024]{1,0:T(8,128...) custom-call(s32[4]{0:T(128)} %len_hbm.1, bf16[128,1024]{1,0:T(8,128)(2,1)} %k_hbm.1, ...), custom_call_target="tpu_custom_call" | custom-call | flops 1048576 | bytes 1024 | tf_op jit(solution)/shard_map/pallas_call | solution.py:340
  1.8 3.7 %collective-permute-start.2 = (bf16[128,1024]{1,0:T(8,128)(2,1)S(1)}, bf16[128,1024]{1,0:T(8,128)(2,1)S(1)}, u32[]{:S(2)}, u32[]{:S(2)}) collective-permute-start(bf16[128,1024]{1,0:T(8,128)(2,1)S(1)} %get-tuple-element.30), channel_id=1, source_target_pairs={{1,2},{2,1},{3,4},{4,3},{5,6},{6,5},{7,8},{8,7},{9,10},{10,9},{11,... | collective-permute-start | bytes 786440 | tf_op jit(solution)/shard_map/ppermute | solution.py:348
  5.5 0.7 %collective-permute-start.3 = (bf16[112,1024]{1,0:T(8,128)(2,1)S(1)}, bf16[112,1024]{1,0:T(8,128)(2,1)S(1)}, u32[]{:S(2)}, u32[]{:S(2)}) collective-permute-start(bf16[112,1024]{1,0:T(8,128)(2,1)S(1)} %get-tuple-element.32), channel_id=1, source_target_pairs={{0,1},{1,0},{2,3},{3,2},{4,5},{5,4},{6,7},{7,6},{8,9},{9,8},{10,11... | collective-permute-start | bytes 688136 | tf_op jit(solution)/shard_map/ppermute | solution.py:349
  6.2 0.0 copy-done.1
  6.2 0.0 copy-done
  6.2 0.7 %shard_map.77 = (bf16[136,768]{1,0:T(8,128)(2,1)S(1)}, bf16[128,256]{1,0:T(8,128)(2,1)S(1)}, bf16[80,1024]{1,0:T(8,128)(2,1)S(1)}, bf16[72,1024]{1,0:T(8,128)(2,1)S(1)}) custom-call(f32[128,128]{1,0:T(8,128)S(1)} %get-tuple-element.27.bias_ref, bf16[128,1024]{1,0:T(8,128)(2,1)S(1)} %copy-done, bf16[128,1024]{1,0:T(8,128)(2,1)S(1)} %get-tuple-element.25.k_ref, ...), custom_call_target="tpu_custom_call" | custom-call | flops 268435456 | bytes 262144 | tf_op jit(solution)/shard_map/pallas_call | solution.py:352
  7.0 0.1 collective-permute-start.4
  7.1 0.5 %collective-permute-start.5 = (bf16[72,1024]{1,0:T(8,128)(2,1)S(1)}, bf16[72,1024]{1,0:T(8,128)(2,1)S(1)}, u32[]{:S(2)}, u32[]{:S(2)}) collective-permute-start(bf16[72,1024]{1,0:T(8,128)(2,1)S(1)} %get-tuple-element.34), channel_id=1, source_target_pairs={{0,1},{1,0},{2,3},{3,2},{4,5},{5,4},{6,7},{7,6},{8,9},{9,8},{10,11... | collective-permute-start | bytes 442376 | tf_op jit(solution)/shard_map/ppermute | solution.py:363
  7.5 2.8 %collective-permute-start.1 = (bf16[136,768]{1,0:T(8,128)(2,1)S(1)}, bf16[136,768]{1,0:T(8,128)(2,1)S(1)}, u32[]{:S(2)}, u32[]{:S(2)}) collective-permute-start(bf16[136,768]{1,0:T(8,128)(2,1)S(1)} %get-tuple-element.29), channel_id=1, source_target_pairs={{1,2},{2,1},{3,4},{4,3},{5,6},{6,5},{7,8},{8,7},{9,10},{10,9},{11,... | collective-permute-start | bytes 626696 | tf_op jit(solution)/shard_map/ppermute | solution.py:360
  10.4 0.0 collective-permute-done.5.gs_ref
  10.4 2.7 %collective-permute-start = (bf16[128,256]{1,0:T(8,128)(2,1)S(1)}, bf16[128,256]{1,0:T(8,128)(2,1)S(1)}, u32[]{:S(2)}, u32[]{:S(2)}) collective-permute-start(bf16[128,256]{1,0:T(8,128)(2,1)S(1)} %get-tuple-element.28), channel_id=1, source_target_pairs={{1,2},{2,1},{3,4},{4,3},{5,6},{6,5},{7,8},{8,7},{9,10},{10,9},{11,... | collective-permute-start | bytes 196616 | tf_op jit(solution)/shard_map/ppermute | solution.py:361
  13.1 0.0 collective-permute-done.4.qn_ref
  13.1 0.0 collective-permute-done.3.kv_ref
  13.1 1.8 %shard_map.78 = (bf16[64,1024]{1,0:T(8,128)(2,1)S(1)}, f32[128,1024]{1,0:T(8,128)S(1)}, f32[128,1024]{1,0:T(8,128)S(1)}) custom-call(f32[256,128]{1,0:T(8,128)S(1)} %get-tuple-element.31.bias_ref, bf16[128,1024]{1,0:T(8,128)(2,1)S(1)} %copy-done, bf16[128,1024]{1,0:T(8,128)(2,1)S(1)} %get-tuple-element.25.k_ref, ...), custom_call_target="tpu_custom_call" | custom-call | bytes 1 | tf_op jit(solution)/shard_map/pallas_call | solution.py:365
  14.9 0.0 collective-permute-done.2.kv_ref
  14.9 1.4 %shard_map.79 = (bf16[64,1024]{1,0:T(8,128)(2,1)S(1)}, bf16[64,1024]{1,0:T(8,128)(2,1)S(1)}, bf16[64,1024]{1,0:T(8,128)(2,1)S(1)}, f32[64,1024]{1,0:T(8,128)S(1)}, f32[64,1024]{1,0:T(8,128)S(1)}) custom-call(f32[256,128]{1,0:T(8,128)S(1)} %get-tuple-element.24.bias_ref, bf16[128,1024]{1,0:T(8,128)(2,1)S(1)} %copy-done, ...), custom_call_target="tpu_custom_call" | custom-call | flops 2147483648 | bytes 2097152 | tf_op jit(solution)/shard_map/pallas_call | solution.py:368
  16.3 0.6 %collective-permute-done.1.qs_ref.st_ref = bf16[136,768]{1,0:T(8,128)(2,1)S(1)} collective-permute-done((bf16[136,768]{1,0:T(8,128)(2,1)S(1)}, bf16[136,768]{1,0:T(8,128)(2,1)S(1)}, u32[]{:S(2)}, u32[]{:S(2)}) %collective-permute-start.1) | collective-permute-done | bytes 208928 | tf_op jit(solution)/shard_map/ppermute | solution.py:360
  16.9 0.6 %shard_map.80 = (bf16[64,768]{1,0:T(8,128)(2,1)S(1)}, bf16[64,768]{1,0:T(8,128)(2,1)S(1)}) custom-call(f32[256,128]{1,0:T(8,128)S(1)} %get-tuple-element.24.bias_ref, bf16[128,1024]{1,0:T(8,128)(2,1)S(1)} %get-tuple-element.25.k_ref, bf16[128,1024]{1,0:T(8,128)(2,1)S(1)} %get-tuple-element.26.v_ref, ...), custom_call_target="tpu_custom_call" | custom-call | bytes 1 | tf_op jit(solution)/shard_map/pallas_call | solution.py:372
  17.5 0.8 %collective-permute-done.qs_ref = bf16[128,256]{1,0:T(8,128)(2,1)S(1)} collective-permute-done((bf16[128,256]{1,0:T(8,128)(2,1)S(1)}, bf16[128,256]{1,0:T(8,128)(2,1)S(1)}, u32[]{:S(2)}, u32[]{:S(2)}) %collective-permute-start) | collective-permute-done | bytes 65568 | tf_op jit(solution)/shard_map/ppermute | solution.py:361
  18.3 1.2 %shard_map.81 = (bf16[128,1024]{1,0:T(8,128)(2,1)}, bf16[128,1024]{1,0:T(8,128)(2,1)}, bf16[128,1024]{1,0:T(8,128)(2,1)}) custom-call(f32[256,128]{1,0:T(8,128)S(1)} %get-tuple-element.24.bias_ref, bf16[128,1024]{1,0:T(8,128)(2,1)S(1)} %get-tuple-element.25.k_ref, bf16[128,1024]{1,0:T(8,128)(2,1)S(1)} %get-tuple-element.26.v_ref, ...), custom_call_target="tpu_custom_call" | custom-call | flops 134217728 | bytes 131072 | tf_op jit(solution)/shard_map/pallas_call | solution.py:374
Async XLA Ops:
  0.6 5.6 %copy-start.1 = (bf16[128,1024]{1,0:T(8,128)(2,1)S(1)}, bf16[128,1024]{1,0:T(8,128)(2,1)}, u32[]{:S(2)}) copy-start(bf16[128,1024]{1,0:T(8,128)(2,1)} %g_ref.5) | copy-start | bytes 786436
  0.6 5.6 %copy-start = (bf16[128,1024]{1,0:T(8,128)(2,1)S(1)}, bf16[128,1024]{1,0:T(8,128)(2,1)}, u32[]{:S(2)}) copy-start(bf16[128,1024]{1,0:T(8,128)(2,1)} %q_ref.5) | copy-start | bytes 786436
  1.8 13.1 %collective-permute-start.2 = (bf16[128,1024]{1,0:T(8,128)(2,1)S(1)}, bf16[128,1024]{1,0:T(8,128)(2,1)S(1)}, u32[]{:S(2)}, u32[]{:S(2)}) collective-permute-start(bf16[128,1024]{1,0:T(8,128)(2,1)S(1)} %get-tuple-element.30), channel_id=1, source_target_pairs={{1,2},{2,1},{3,4},{4,3},{5,6},{6,5},{7,8},{8,7},{9,10},{10,9},{11,... | collective-permute-start | bytes 786440 | tf_op jit(solution)/shard_map/ppermute | solution.py:348
  5.5 7.6 %collective-permute-start.3 = (bf16[112,1024]{1,0:T(8,128)(2,1)S(1)}, bf16[112,1024]{1,0:T(8,128)(2,1)S(1)}, u32[]{:S(2)}, u32[]{:S(2)}) collective-permute-start(bf16[112,1024]{1,0:T(8,128)(2,1)S(1)} %get-tuple-element.32), channel_id=1, source_target_pairs={{0,1},{1,0},{2,3},{3,2},{4,5},{5,4},{6,7},{7,6},{8,9},{9,8},{10,11... | collective-permute-start | bytes 688136 | tf_op jit(solution)/shard_map/ppermute | solution.py:349
  7.0 6.1 %collective-permute-start.4 = (bf16[80,1024]{1,0:T(8,128)(2,1)S(1)}, bf16[80,1024]{1,0:T(8,128)(2,1)S(1)}, u32[]{:S(2)}, u32[]{:S(2)}) collective-permute-start(bf16[80,1024]{1,0:T(8,128)(2,1)S(1)} %get-tuple-element.33), channel_id=1, source_target_pairs={{0,1},{1,0},{2,3},{3,2},{4,5},{5,4},{6,7},{7,6},{8,9},{9,8},{10,11... | collective-permute-start | bytes 491528 | tf_op jit(solution)/shard_map/ppermute | solution.py:362
  7.1 3.3 %collective-permute-start.5 = (bf16[72,1024]{1,0:T(8,128)(2,1)S(1)}, bf16[72,1024]{1,0:T(8,128)(2,1)S(1)}, u32[]{:S(2)}, u32[]{:S(2)}) collective-permute-start(bf16[72,1024]{1,0:T(8,128)(2,1)S(1)} %get-tuple-element.34), channel_id=1, source_target_pairs={{0,1},{1,0},{2,3},{3,2},{4,5},{5,4},{6,7},{7,6},{8,9},{9,8},{10,11... | collective-permute-start | bytes 442376 | tf_op jit(solution)/shard_map/ppermute | solution.py:363
  7.5 9.3 %collective-permute-start.1 = (bf16[136,768]{1,0:T(8,128)(2,1)S(1)}, bf16[136,768]{1,0:T(8,128)(2,1)S(1)}, u32[]{:S(2)}, u32[]{:S(2)}) collective-permute-start(bf16[136,768]{1,0:T(8,128)(2,1)S(1)} %get-tuple-element.29), channel_id=1, source_target_pairs={{1,2},{2,1},{3,4},{4,3},{5,6},{6,5},{7,8},{8,7},{9,10},{10,9},{11,... | collective-permute-start | bytes 626696 | tf_op jit(solution)/shard_map/ppermute | solution.py:360
  10.4 7.9 %collective-permute-start = (bf16[128,256]{1,0:T(8,128)(2,1)S(1)}, bf16[128,256]{1,0:T(8,128)(2,1)S(1)}, u32[]{:S(2)}, u32[]{:S(2)}) collective-permute-start(bf16[128,256]{1,0:T(8,128)(2,1)S(1)} %get-tuple-element.28), channel_id=1, source_target_pairs={{1,2},{2,1},{3,4},{4,3},{5,6},{6,5},{7,8},{8,7},{9,10},{10,9},{11,... | collective-permute-start | bytes 196616 | tf_op jit(solution)/shard_map/ppermute | solution.py:361

commit v6 on v5

--- a/solution.py
+++ b/solution.py
@@ -220,9 +220,13 @@
     edge(rs, pairs_of(0, cols), 0, bias_ref, k_ref, v_ref, qn_ref.at[:half], gs_ref.at[:half], stats, add)
 
 
-def across_kernel(bias_ref, q_ref, k_ref, v_ref, g_ref, kv_ref, dka_ref, dva_ref, dq_ref, dkn_ref, dvn_ref, dk_ref, dv_ref):
+def across_kernel(
+    bias_ref, q_ref, k_ref, v_ref, g_ref, kv_ref, dka_ref, dva_ref, dqn, dq_out, dq_ref, dkn_ref, dvn_ref, dk_ref, dv_ref, sem
+):
     rows, cols = k_ref.shape
     half = rows // 2
+    copy = pltpu.make_async_copy(dqn, dq_out.at[side_rows(False, half)], sem)
+    copy.start()
     odd = lax.rem(flat_index(), 2)
 
     def put(cs, dk, dv):
@@ -245,6 +249,7 @@
         dq_ref,
         put,
     )
+    copy.wait()
 
 
 def edge_into(first, bias_ref, k_ref, v_ref, qs_ref, st_ref, dka_ref, dva_ref, dk_ref, dv_ref):
@@ -283,14 +288,13 @@
 
 
 def last_kernel(
-    bias_ref, k_ref, v_ref, qs_ref, st_ref, dka_ref, dva_ref, dqn, dqm, dkn, dvn, dk1, dv1, dq_out, dk_out, dv_out, dk2, dv2, sems
+    bias_ref, k_ref, v_ref, qs_ref, st_ref, dka_ref, dva_ref, dqm, dkn, dvn, dk1, dv1, dq_in, dq_out, dk_out, dv_out, dk2, dv2, sems
 ):
     rows, cols = k_ref.shape
     half = rows // 2
     mine, other = side_rows(True, half), side_rows(False, half)
     first = cols - qs_ref.shape[1]
     early = [
-        (dqn, dq_out.at[other]),
         (dqm, dq_out.at[mine]),
         (dkn, dk_out.at[other]),
         (dvn, dv_out.at[other]),
@@ -326,13 +330,14 @@
     masks = sds((2 * rows, rows), F32)
     dma = pltpu.SemaphoreType.DMA((3,))
 
-    def call(kernel, out_shape, in_specs, out_specs, scratch, flops):
+    def call(kernel, out_shape, in_specs, out_specs, scratch, flops, alias={}):
         return pl.pallas_call(
             kernel,
             out_shape=out_shape,
             in_specs=in_specs,
             out_specs=out_specs,
             scratch_shapes=scratch,
+            input_output_aliases=alias,
             compiler_params=pltpu.CompilerParams(vmem_limit_bytes=20 << 20),
             cost_estimate=pl.CostEstimate(flops=flops, bytes_accessed=max(flops >> 10, 1), transcendentals=0),
         )
@@ -365,15 +370,17 @@
     dqn, dk, dv = call(within_kernel, (low_s, acc, acc), [VM] * 8, (VM,) * 3, [], COSTS[1])(
         bias_e, q, k, v, g, kv_e, q_e, gs_e
     )
-    dqm, dkn, dvn, dk, dv = call(across_kernel, (low_s,) * 3 + (part,) * 2, [VM] * 8, (VM,) * 5, [], COSTS[2])(
-        bias_o, q, k, v, g, kv_o, dk, dv
+    dq, dqm, dkn, dvn, dk, dv = call(
+        across_kernel, (whole,) + (low_s,) * 3 + (part,) * 2, [VM] * 9, (HB,) + (VM,) * 5, [pltpu.SemaphoreType.DMA], COSTS[2]
+    )(
+        bias_o, q, k, v, g, kv_o, dk, dv, dqn
     )
     done = sds((half, cut), BF16)
     dk1, dv1 = call(first_edge_kernel, (done, done), [VM] * 6, (VM,) * 2, [], COSTS[3])(bias_o, k, v, qs_1, dk, dv)
     rest = pltpu.VMEM((half, cols - cut), BF16)
     return call(
-        last_kernel, (whole,) * 3, [VM] * 13, (HB,) * 3, [rest, rest, pltpu.SemaphoreType.DMA((8,))], COSTS[4]
-    )(bias_o, k, v, qs_2, qs_1, dk, dv, dqn, dqm, dkn, dvn, dk1, dv1)
+        last_kernel, (whole,) * 3, [VM] * 12 + [HB], (HB,) * 3, [rest, rest, pltpu.SemaphoreType.DMA((7,))], COSTS[4], {12: 0}
+    )(bias_o, k, v, qs_2, qs_1, dk, dv, dqm, dkn, dvn, dk1, dv1, dq)
 
 
 def solution(mesh):

time: 19.6 us -> 19.6 us (level)
  no operation moved by 1% of the time
where the time goes in v6:
time: 19.6 us; the launch traced here: 19.4 us
  starting transfers between devices  10.5 us (54%)
  Pallas kernels  6.7 us (34%)
  waiting for transfers between devices  1.4 us (7%)
  between operations  0.74 us (4%)
    ppermute x1, starting transfers between devices, body(): kv_o = lax.ppermute(kv_o, AXES, across)  3.71 us
    ppermute x1, starting transfers between devices, body(): qs_1 = lax.ppermute(qs_1, AXES, across)  2.8 us
    ppermute x1, starting transfers between devices, body(): qs_2 = lax.ppermute(qs_2, AXES, across)  2.75 us
    pallas_call x1, Pallas kernels, body(): call(within_kernel, (low_s, acc, acc), [VM] * 8, (VM,) * 3, [], COSTS[1])  1.79 us
    pallas_call x1, Pallas kernels, body(): call(across_kernel, (whole,) + (low_s,) * 3 + (part,) * 2, [VM] * 9, (HB,...  1.37 us
    pallas_call x1, Pallas kernels, body(): call(prep_kernel, (whole,) * 3 + (sds((rows - MOVED, cols), BF16), sds((r...  1.13 us
    pallas_call x1, Pallas kernels, body(): call(last_kernel, (whole,) * 3, [VM] * 12 + [HB], (HB,) * 3, [rest, rest,...  1.1 us
    ppermute x1, waiting for transfers between devices, body(): qs_2 = lax.ppermute(qs_2, AXES, across)  0.83 us
  transfers between devices with their start and end apart: 6, of which 2 were waited for; matrix products, arithmetic and copies ran while one was open for 0% of the time, Pallas kernels for 23%

profile of v6, /device:TPU:25, one launch (start us, length us, event | category | flops | bytes accessed | tf_op | source)
XLA Modules:
  0.0 19.4 jit_solution(2084723470110767428)
XLA Ops:
  0.6 0.0 copy-start.1
  0.6 0.0 copy-start
  0.7 1.1 %shard_map.76 = (bf16[128,1024]{1,0:T(8,128)(2,1)S(1)}, bf16[128,1024]{1,0:T(8,128)(2,1)S(1)}, bf16[128,1024]{1,0:T(8,128)(2,1)S(1)}, bf16[112,1024]{1,0:T(8,128...) custom-call(s32[4]{0:T(128)} %len_hbm.1, bf16[128,1024]{1,0:T(8,128)(2,1)} %k_hbm.1, ...), custom_call_target="tpu_custom_call" | custom-call | flops 1048576 | bytes 1024 | tf_op jit(solution)/shard_map/pallas_call | solution.py:345
  1.8 3.7 %collective-permute-start.2 = (bf16[128,1024]{1,0:T(8,128)(2,1)S(1)}, bf16[128,1024]{1,0:T(8,128)(2,1)S(1)}, u32[]{:S(2)}, u32[]{:S(2)}) collective-permute-start(bf16[128,1024]{1,0:T(8,128)(2,1)S(1)} %get-tuple-element.31), channel_id=1, source_target_pairs={{1,2},{2,1},{3,4},{4,3},{5,6},{6,5},{7,8},{8,7},{9,10},{10,9},{11,... | collective-permute-start | bytes 786440 | tf_op jit(solution)/shard_map/ppermute | solution.py:353
  5.5 0.7 %collective-permute-start.3 = (bf16[112,1024]{1,0:T(8,128)(2,1)S(1)}, bf16[112,1024]{1,0:T(8,128)(2,1)S(1)}, u32[]{:S(2)}, u32[]{:S(2)}) collective-permute-start(bf16[112,1024]{1,0:T(8,128)(2,1)S(1)} %get-tuple-element.33), channel_id=1, source_target_pairs={{0,1},{1,0},{2,3},{3,2},{4,5},{5,4},{6,7},{7,6},{8,9},{9,8},{10,11... | collective-permute-start | bytes 688136 | tf_op jit(solution)/shard_map/ppermute | solution.py:354
  6.2 0.0 copy-done.1
  6.2 0.0 copy-done
  6.2 0.7 %shard_map.77 = (bf16[136,768]{1,0:T(8,128)(2,1)S(1)}, bf16[128,256]{1,0:T(8,128)(2,1)S(1)}, bf16[80,1024]{1,0:T(8,128)(2,1)S(1)}, bf16[72,1024]{1,0:T(8,128)(2,1)S(1)}) custom-call(f32[128,128]{1,0:T(8,128)S(1)} %get-tuple-element.28.bias_ref, bf16[128,1024]{1,0:T(8,128)(2,1)S(1)} %copy-done, bf16[128,1024]{1,0:T(8,128)(2,1)S(1)} %get-tuple-element.26.k_ref, ...), custom_call_target="tpu_custom_call" | custom-call | flops 268435456 | bytes 262144 | tf_op jit(solution)/shard_map/pallas_call | solution.py:357
  7.0 0.1 collective-permute-start.4
  7.1 0.5 %collective-permute-start.5 = (bf16[72,1024]{1,0:T(8,128)(2,1)S(1)}, bf16[72,1024]{1,0:T(8,128)(2,1)S(1)}, u32[]{:S(2)}, u32[]{:S(2)}) collective-permute-start(bf16[72,1024]{1,0:T(8,128)(2,1)S(1)} %get-tuple-element.35), channel_id=1, source_target_pairs={{0,1},{1,0},{2,3},{3,2},{4,5},{5,4},{6,7},{7,6},{8,9},{9,8},{10,11... | collective-permute-start | bytes 442376 | tf_op jit(solution)/shard_map/ppermute | solution.py:368
  7.5 2.8 %collective-permute-start.1 = (bf16[136,768]{1,0:T(8,128)(2,1)S(1)}, bf16[136,768]{1,0:T(8,128)(2,1)S(1)}, u32[]{:S(2)}, u32[]{:S(2)}) collective-permute-start(bf16[136,768]{1,0:T(8,128)(2,1)S(1)} %get-tuple-element.30), channel_id=1, source_target_pairs={{1,2},{2,1},{3,4},{4,3},{5,6},{6,5},{7,8},{8,7},{9,10},{10,9},{11,... | collective-permute-start | bytes 626696 | tf_op jit(solution)/shard_map/ppermute | solution.py:365
  10.3 0.0 collective-permute-done.5.gs_ref
  10.4 2.8 %collective-permute-start = (bf16[128,256]{1,0:T(8,128)(2,1)S(1)}, bf16[128,256]{1,0:T(8,128)(2,1)S(1)}, u32[]{:S(2)}, u32[]{:S(2)}) collective-permute-start(bf16[128,256]{1,0:T(8,128)(2,1)S(1)} %get-tuple-element.29), channel_id=1, source_target_pairs={{1,2},{2,1},{3,4},{4,3},{5,6},{6,5},{7,8},{8,7},{9,10},{10,9},{11,... | collective-permute-start | bytes 196616 | tf_op jit(solution)/shard_map/ppermute | solution.py:366
  13.1 0.0 collective-permute-done.4.qn_ref
  13.1 0.0 collective-permute-done.3.kv_ref
  13.1 1.8 %shard_map.78 = (bf16[64,1024]{1,0:T(8,128)(2,1)S(1)}, f32[128,1024]{1,0:T(8,128)S(1)}, f32[128,1024]{1,0:T(8,128)S(1)}) custom-call(f32[256,128]{1,0:T(8,128)S(1)} %get-tuple-element.32.bias_ref, bf16[128,1024]{1,0:T(8,128)(2,1)S(1)} %copy-done, bf16[128,1024]{1,0:T(8,128)(2,1)S(1)} %get-tuple-element.26.k_ref, ...), custom_call_target="tpu_custom_call" | custom-call | bytes 1 | tf_op jit(solution)/shard_map/pallas_call | solution.py:370
  14.9 0.0 collective-permute-done.2.kv_ref
  14.9 1.4 %shard_map.79 = (bf16[128,1024]{1,0:T(8,128)(2,1)}, bf16[64,1024]{1,0:T(8,128)(2,1)S(1)}, bf16[64,1024]{1,0:T(8,128)(2,1)S(1)}, bf16[64,1024]{1,0:T(8,128)(2,1)S...) custom-call(f32[256,128]{1,0:T(8,128)S(1)} %get-tuple-element.25.bias_ref, bf16[128,1024]{1,0:T(8,128)(2,1)S(1)} %copy-done, ...), custom_call_target="tpu_custom_call" | custom-call | flops 2147483648 | bytes 2097152 | tf_op jit(solution)/shard_map/pallas_call | solution.py:373
  16.3 0.6 %collective-permute-done.1.qs_ref.st_ref = bf16[136,768]{1,0:T(8,128)(2,1)S(1)} collective-permute-done((bf16[136,768]{1,0:T(8,128)(2,1)S(1)}, bf16[136,768]{1,0:T(8,128)(2,1)S(1)}, u32[]{:S(2)}, u32[]{:S(2)}) %collective-permute-start.1) | collective-permute-done | bytes 208928 | tf_op jit(solution)/shard_map/ppermute | solution.py:365
  16.9 0.6 %shard_map.80 = (bf16[64,768]{1,0:T(8,128)(2,1)S(1)}, bf16[64,768]{1,0:T(8,128)(2,1)S(1)}) custom-call(f32[256,128]{1,0:T(8,128)S(1)} %get-tuple-element.25.bias_ref, bf16[128,1024]{1,0:T(8,128)(2,1)S(1)} %get-tuple-element.26.k_ref, bf16[128,1024]{1,0:T(8,128)(2,1)S(1)} %get-tuple-element.27.v_ref, ...), custom_call_target="tpu_custom_call" | custom-call | bytes 1 | tf_op jit(solution)/shard_map/pallas_call | solution.py:379
  17.5 0.8 %collective-permute-done.qs_ref = bf16[128,256]{1,0:T(8,128)(2,1)S(1)} collective-permute-done((bf16[128,256]{1,0:T(8,128)(2,1)S(1)}, bf16[128,256]{1,0:T(8,128)(2,1)S(1)}, u32[]{:S(2)}, u32[]{:S(2)}) %collective-permute-start) | collective-permute-done | bytes 65568 | tf_op jit(solution)/shard_map/ppermute | solution.py:366
  18.3 1.1 %shard_map.81 = (bf16[128,1024]{1,0:T(8,128)(2,1)}, bf16[128,1024]{1,0:T(8,128)(2,1)}, bf16[128,1024]{1,0:T(8,128)(2,1)}) custom-call(f32[256,128]{1,0:T(8,128)S(1)} %get-tuple-element.25.bias_ref, bf16[128,1024]{1,0:T(8,128)(2,1)S(1)} %get-tuple-element.26.k_ref, bf16[128,1024]{1,0:T(8,128)(2,1)S(1)} %get-tuple-element.27.v_ref, ...), custom_call_target="tpu_custom_call", output_to_operand_aliasing={{0}: (12, {})} | custom-call | flops 134217728 | bytes 131072 | tf_op jit(solution)/shard_map/pallas_call | solution.py:381
Async XLA Ops:
  0.6 5.6 %copy-start.1 = (bf16[128,1024]{1,0:T(8,128)(2,1)S(1)}, bf16[128,1024]{1,0:T(8,128)(2,1)}, u32[]{:S(2)}) copy-start(bf16[128,1024]{1,0:T(8,128)(2,1)} %g_ref.5) | copy-start | bytes 786436
  0.6 5.6 %copy-start = (bf16[128,1024]{1,0:T(8,128)(2,1)S(1)}, bf16[128,1024]{1,0:T(8,128)(2,1)}, u32[]{:S(2)}) copy-start(bf16[128,1024]{1,0:T(8,128)(2,1)} %q_ref.5) | copy-start | bytes 786436
  1.8 13.1 %collective-permute-start.2 = (bf16[128,1024]{1,0:T(8,128)(2,1)S(1)}, bf16[128,1024]{1,0:T(8,128)(2,1)S(1)}, u32[]{:S(2)}, u32[]{:S(2)}) collective-permute-start(bf16[128,1024]{1,0:T(8,128)(2,1)S(1)} %get-tuple-element.31), channel_id=1, source_target_pairs={{1,2},{2,1},{3,4},{4,3},{5,6},{6,5},{7,8},{8,7},{9,10},{10,9},{11,... | collective-permute-start | bytes 786440 | tf_op jit(solution)/shard_map/ppermute | solution.py:353
  5.5 7.6 %collective-permute-start.3 = (bf16[112,1024]{1,0:T(8,128)(2,1)S(1)}, bf16[112,1024]{1,0:T(8,128)(2,1)S(1)}, u32[]{:S(2)}, u32[]{:S(2)}) collective-permute-start(bf16[112,1024]{1,0:T(8,128)(2,1)S(1)} %get-tuple-element.33), channel_id=1, source_target_pairs={{0,1},{1,0},{2,3},{3,2},{4,5},{5,4},{6,7},{7,6},{8,9},{9,8},{10,11... | collective-permute-start | bytes 688136 | tf_op jit(solution)/shard_map/ppermute | solution.py:354
  7.0 6.1 %collective-permute-start.4 = (bf16[80,1024]{1,0:T(8,128)(2,1)S(1)}, bf16[80,1024]{1,0:T(8,128)(2,1)S(1)}, u32[]{:S(2)}, u32[]{:S(2)}) collective-permute-start(bf16[80,1024]{1,0:T(8,128)(2,1)S(1)} %get-tuple-element.34), channel_id=1, source_target_pairs={{0,1},{1,0},{2,3},{3,2},{4,5},{5,4},{6,7},{7,6},{8,9},{9,8},{10,11... | collective-permute-start | bytes 491528 | tf_op jit(solution)/shard_map/ppermute | solution.py:367
  7.1 3.3 %collective-permute-start.5 = (bf16[72,1024]{1,0:T(8,128)(2,1)S(1)}, bf16[72,1024]{1,0:T(8,128)(2,1)S(1)}, u32[]{:S(2)}, u32[]{:S(2)}) collective-permute-start(bf16[72,1024]{1,0:T(8,128)(2,1)S(1)} %get-tuple-element.35), channel_id=1, source_target_pairs={{0,1},{1,0},{2,3},{3,2},{4,5},{5,4},{6,7},{7,6},{8,9},{9,8},{10,11... | collective-permute-start | bytes 442376 | tf_op jit(solution)/shard_map/ppermute | solution.py:368
  7.5 9.3 %collective-permute-start.1 = (bf16[136,768]{1,0:T(8,128)(2,1)S(1)}, bf16[136,768]{1,0:T(8,128)(2,1)S(1)}, u32[]{:S(2)}, u32[]{:S(2)}) collective-permute-start(bf16[136,768]{1,0:T(8,128)(2,1)S(1)} %get-tuple-element.30), channel_id=1, source_target_pairs={{1,2},{2,1},{3,4},{4,3},{5,6},{6,5},{7,8},{8,7},{9,10},{10,9},{11,... | collective-permute-start | bytes 626696 | tf_op jit(solution)/shard_map/ppermute | solution.py:365
  10.4 7.9 %collective-permute-start = (bf16[128,256]{1,0:T(8,128)(2,1)S(1)}, bf16[128,256]{1,0:T(8,128)(2,1)S(1)}, u32[]{:S(2)}, u32[]{:S(2)}) collective-permute-start(bf16[128,256]{1,0:T(8,128)(2,1)S(1)} %get-tuple-element.29), channel_id=1, source_target_pairs={{1,2},{2,1},{3,4},{4,3},{5,6},{6,5},{7,8},{8,7},{9,10},{10,9},{11,... | collective-permute-start | bytes 196616 | tf_op jit(solution)/shard_map/ppermute | solution.py:366
